TPU v7x, 128 devices: a whole 4x4x4 slice. The times are simulated.
128 devices in a mesh: view: 4 (over y_hi, core), tile: 32 (over z, y_lo, x).
Axes of the slice: x: 4, y: 4 (y_hi: 2, y_lo: 2; y = y_hi * 2 + y_lo), z: 4, core: 2. Of those that a mesh axis runs over, the one named last changes fastest.
Arguments:
- objects: float32 [4, 2, 128, 1024], P('view', None, None, 'tile'), may hold values from -6 to 6
- probe: float32 [2, 128, 128], replicated, may hold values from -0.75 to 0.75
- positions: int32 [4, 256], P('view', 'tile'), may hold values from 0 to 896, as said below
- amplitudes: float32 [4, 256, 128, 128], P('view', 'tile'), may hold values from 0 to 0.53033006
- reproj_prev: float32 [4, 2, 128, 1024], P('view', None, None, 'tile'), may hold values from -6 to 6
- multipliers: float32 [4, 2, 128, 1024], P('view', None, None, 'tile'), may hold values from -4 to 4
- volume: float32 [2, 128, 1024, 1024], P(None, ('view', 'tile')), may hold values from -6 to 6
- angles: int32 [4], replicated, may hold values from 0 to 3
- penalty: int32 [2], replicated, may hold values from 1 to 5, as said below
Outputs:
- reprojections: float32 [4, 2, 128, 1024], P('view', None, None, 'tile')
- new_multipliers: float32 [4, 2, 128, 1024], P('view', None, None, 'tile')
Inputs may be any that keep to these rules, and one draw needn't show every extreme that they name: `positions`: the window of a scan covers 128 columns inside the strip. The penalty is the first entry divided by the second; the first is 1 to 4, the second is 5. `angles`: angle index k is a view at k times 90 degrees.
All inputs are finite; a program needn't handle non-finite values.
Results may differ from a plain program's by a relative error of at most 0.0001.
Values sent between devices are 32-bit elements; how exact they have to be, the bound alone decides.
A program may use at most 64 MiB of HBM per device.

v0:
```python
import math

import jax
import jax.numpy as jnp
from jax import lax
from jax.sharding import PartitionSpec as P

ITERS = 2


HIGHEST = lax.Precision.HIGHEST


def dft_tables(length):
    indices = jnp.arange(length, dtype=jnp.int32)
    phase = (indices[:, None] * indices[None, :] % length).astype(jnp.float32) * (
        2.0 * math.pi / length
    )
    factor = 1.0 / math.sqrt(length)
    return (jnp.cos(phase) * factor, -jnp.sin(phase) * factor)


def left_apply(cosine, sine, sign, real_part, imag_part):
    first = jnp.einsum("rk,nkc->nrc", cosine, real_part, precision=HIGHEST)
    second = jnp.einsum("rk,nkc->nrc", sine, imag_part, precision=HIGHEST)
    third = jnp.einsum("rk,nkc->nrc", cosine, imag_part, precision=HIGHEST)
    fourth = jnp.einsum("rk,nkc->nrc", sine, real_part, precision=HIGHEST)
    return (first - sign * second, third + sign * fourth)


def right_apply(cosine, sine, sign, real_part, imag_part):
    first = jnp.einsum("nrk,kc->nrc", real_part, cosine, precision=HIGHEST)
    second = jnp.einsum("nrk,kc->nrc", imag_part, sine, precision=HIGHEST)
    third = jnp.einsum("nrk,kc->nrc", imag_part, cosine, precision=HIGHEST)
    fourth = jnp.einsum("nrk,kc->nrc", real_part, sine, precision=HIGHEST)
    return (first - sign * second, third + sign * fourth)


def window_columns(starts, width):
    return (starts[:, None] + jnp.arange(width, dtype=jnp.int32)[None, :]).reshape(-1)


def strip_gradient(strip, starts, measured, probe, floor):
    rows = strip.shape[1]
    width = probe.shape[2]
    total = strip.shape[2]
    windows = jax.vmap(lambda start: lax.dynamic_slice_in_dim(strip, start, width, axis=2))(starts)
    window_re = windows[:, 0]
    window_im = windows[:, 1]
    probe_re = probe[0]
    probe_im = probe[1]
    exit_re = probe_re * window_re - probe_im * window_im
    exit_im = probe_re * window_im + probe_im * window_re
    row_cos, row_sin = dft_tables(rows)
    col_cos, col_sin = dft_tables(width)
    mid_re, mid_im = left_apply(row_cos, row_sin, 1.0, exit_re, exit_im)
    far_re, far_im = right_apply(col_cos, col_sin, 1.0, mid_re, mid_im)
    modulus = jnp.sqrt(far_re * far_re + far_im * far_im)
    keep = 1.0 - measured / jnp.maximum(modulus, floor)
    back_re, back_im = left_apply(row_cos, row_sin, -1.0, far_re * keep, far_im * keep)
    back_re, back_im = right_apply(col_cos, col_sin, -1.0, back_re, back_im)
    grad_re = probe_re * back_re + probe_im * back_im
    grad_im = probe_re * back_im - probe_im * back_re
    columns = window_columns(starts, width)
    values = jnp.stack([grad_re, grad_im], axis=0).transpose(0, 2, 1, 3).reshape(2, rows, -1)
    return jnp.zeros((2, rows, total), jnp.float32).at[:, :, columns].add(values)


def illumination(starts, probe, total):
    rows = probe.shape[1]
    width = probe.shape[2]
    power = probe[0] * probe[0] + probe[1] * probe[1]
    values = jnp.broadcast_to(power[:, None, :], (rows, starts.shape[0], width)).reshape(rows, -1)
    return jnp.zeros((rows, total), jnp.float32).at[:, window_columns(starts, width)].add(values)


def project(column_sum, row_sum, angles):
    length = column_sum.shape[-1]
    angle_grid = angles[:, None]
    along = column_sum[..., None, :]
    across = row_sum[..., None, :]
    result = jnp.where(
        angle_grid == 0,
        along,
        jnp.where(
            angle_grid == 1,
            across,
            jnp.where(angle_grid == 2, jnp.flip(along, -1), jnp.flip(across, -1)),
        ),
    )
    return result * (1.0 / math.sqrt(length))


def backproject(lines, angles):
    length = lines.shape[-1]
    angle_grid = angles[:, None]
    zero = jnp.zeros_like(lines)
    column_term = jnp.sum(jnp.where(angle_grid == 0, lines, zero), -2) + jnp.flip(
        jnp.sum(jnp.where(angle_grid == 2, lines, zero), -2), -1
    )
    row_term = jnp.sum(jnp.where(angle_grid == 1, lines, zero), -2) + jnp.flip(
        jnp.sum(jnp.where(angle_grid == 3, lines, zero), -2), -1
    )
    return (column_term[..., None, :] + row_term[..., :, None]) * (1.0 / math.sqrt(length))


def shards(
    objects, probe, positions, amplitudes, reproj_prev, multipliers, volume, angles, penalty
):
    tiles = lax.axis_size("tile")
    views = lax.axis_size("view")
    strip = objects[0]
    previous = reproj_prev[0]
    lagrange = multipliers[0]
    starts = positions[0]
    measured = amplitudes[0]
    tile_width = strip.shape[2]
    total = tile_width * tiles
    width = probe.shape[2]
    cover = starts.shape[0] * tiles * width // total
    floor = 0.25 / math.sqrt(cover)
    penalty_value = penalty[0].astype(jnp.float32) / penalty[1].astype(jnp.float32)
    power = lax.psum_scatter(
        illumination(starts, probe, total), "tile", scatter_dimension=1, tiled=True
    )
    for sweep in range(ITERS):
        whole = lax.all_gather(strip, "tile", axis=2, tiled=True)
        grad = lax.psum_scatter(
            strip_gradient(whole, starts, measured, probe, floor),
            "tile",
            scatter_dimension=2,
            tiled=True,
        )
        strip = strip - (grad + penalty_value * (strip - previous) + lagrange) / (
            power + penalty_value
        )
    owned = volume.shape[1]
    slabs, slab_lagrange = (
        lax.all_to_all(strip, ("view", "tile"), split_axis=1, concat_axis=2, tiled=True),
        lax.all_to_all(lagrange, ("view", "tile"), split_axis=1, concat_axis=2, tiled=True),
    )
    slabs = slabs.reshape(2, owned, views, total)
    slab_lagrange = slab_lagrange.reshape(2, owned, views, total)
    projected = project(volume.sum(2), volume.sum(3), angles)
    misfit = projected - slabs - slab_lagrange / penalty_value
    updated = volume - backproject(misfit, angles) / views
    fresh = project(updated.sum(2), updated.sum(3), angles)
    renewed = slab_lagrange + penalty_value * (slabs - fresh)
    fresh_strip, renewed_strip = (
        lax.all_to_all(
            fresh.reshape(2, owned, views * total),
            ("view", "tile"),
            split_axis=2,
            concat_axis=1,
            tiled=True,
        ),
        lax.all_to_all(
            renewed.reshape(2, owned, views * total),
            ("view", "tile"),
            split_axis=2,
            concat_axis=1,
            tiled=True,
        ),
    )
    return (fresh_strip[None], renewed_strip[None])


def solution(mesh):
    return jax.shard_map(
        shards,
        mesh=mesh,
        in_specs=(
            P("view", None, None, "tile"),
            P(),
            P("view", "tile"),
            P("view", "tile", None, None),
            P("view", None, None, "tile"),
            P("view", None, None, "tile"),
            P(None, ("view", "tile"), None, None),
            P(),
            P(),
        ),
        out_specs=(P("view", None, None, "tile"), P("view", None, None, "tile")),
        check_vma=False,
    )
```

profile of v0, /device:TPU:9, one launch (start us, length us, event | category | flops | bytes accessed | tf_op | source)
XLA Modules:
  0.0 1270.8 jit_solution(15110685563736691346)
XLA Ops:
  7.2 1.4 copy.347
  8.7 0.9 multiply_add_fusion
  10.4 6.8 scatter_custom_fusion.1
  18.0 0.9 slice_bitcast_fusion.1
  18.9 116.7 %all-gather.6.cloned.1.call-done = f32[1,2,128,1024]{2,1,0,3:T(2,128)} async-done(((f32[1,2,128,32]{2,1,0,3:T(2,128)}), f32[1,2,128,1024]{2,1,0,3:T(2,128)}) %all-gather.6.cloned.1.call-update) | async-done | bytes 1048592 | tf_op jit(solution)/shard_map/all_gather | solution.py:127
  135.6 2.9 gather_fusion
  138.5 1.0 fusion.267
  140.4 1.2 fusion.30
  141.6 1.2 fusion.34
  142.8 1.2 fusion.16
  144.0 1.1 fusion.83
  145.1 1.2 fusion.17
  146.3 1.1 fusion.86
  147.5 1.1 convolution_subtract_fusion.2
  148.6 1.2 fusion.26
  149.9 1.1 fusion.71
  151.0 1.5 fusion.81
  152.5 1.1 fusion.13
  153.7 1.1 fusion.15
  154.8 1.1 fusion.79
  156.0 1.1 fusion.77
  157.1 1.1 fusion.10
  158.3 1.1 add_bitcast_fusion.1
  159.8 0.8 copy.383
  160.9 32.8 %scatter_fusion = f32[2,128,1024]{1,0,2:T(2,128)S(1)} fusion(f32[2,128,1024]{1,0,2:T(2,128)S(1)} %broadcast.548.clone, s32[1024]{0:T(1024)S(1)} %bitcast.288, f32[1024,2,128]{2,1,0:T(2,128)S(1)} %copy.383), kind=kCustom, calls=%fused_computation.2 | custom fusion | flops 262144 | bytes 3149824 | tf_op jit(solution)/shard_map/scatter-add | solution.py:66
  193.7 1.0 copy-done.1
  198.0 96.8 %reduce-scatter.2.cloned.1.call-done = f32[128,32]{0,1:T(8,128)} async-done(((f32[128,1024]{0,1:T(8,128)}), f32[128,32]{0,1:T(8,128)}) %reduce-scatter.2.cloned.1.call-update) | async-done | bytes 16400 | tf_op jit(solution)/shard_map/reduce_scatter | solution.py:123
  295.5 313.4 %all-reduce.6.cloned.1.call-done = f32[2,128,1024]{1,0,2:T(2,128)} async-done(((f32[2,128,1024]{1,0,2:T(2,128)}), f32[2,128,1024]{1,0,2:T(2,128)}) %all-reduce.6.cloned.1.call-update) | async-done | bytes 1048592
  611.1 36.6 %all-to-all-start.1 = ((f32[2,128,32]{2,0,1:T(2,128)}), f32[2,128,32]{2,0,1:T(2,128)S(1)}, u32[]{:S(2)}, u32[]{:S(2)}) async-start(f32[2,128,32]{2,0,1:T(2,128)} %copy.426), calls=%async_computation.2 | async-start | bytes 262144 | tf_op jit(solution)/shard_map/all_to_all | solution.py:140
  647.7 114.6 %all-gather.4.cloned.1.call-done = f32[2,128,1024]{1,0,2:T(2,128)} async-done(((f32[2,128,32]{1,0,2:T(2,128)}), f32[2,128,1024]{1,0,2:T(2,128)}) %all-gather.4.cloned.1.call-update) | async-done | bytes 1048592 | tf_op jit(solution)/shard_map/all_gather | solution.py:127
  762.3 2.9 gather_fusion.1
  765.2 1.0 fusion.266
  767.1 1.2 fusion.36
  768.3 1.2 fusion.40
  769.5 1.2 fusion.8
  770.7 1.1 fusion.65
  771.9 1.2 fusion.9
  773.1 1.1 fusion.68
  774.2 1.1 convolution_subtract_fusion
  775.3 1.2 fusion.24
  776.6 1.1 fusion.61
  777.7 1.3 fusion.63
  779.1 1.1 fusion.5
  780.2 1.1 fusion.7
  781.4 1.1 fusion.75
  782.5 1.1 fusion.73
  783.6 1.1 fusion.2
  784.8 1.1 add_bitcast_fusion
  786.3 0.8 copy.422
  787.4 32.8 %scatter_fusion.1 = f32[2,128,1024]{1,0,2:T(2,128)S(1)} fusion(f32[2,128,1024]{1,0,2:T(2,128)S(1)} %broadcast.548, s32[1024]{0:T(1024)S(1)} %bitcast.289, f32[1024,2,128]{2,1,0:T(2,128)S(1)} %copy.422), kind=kCustom, calls=%fused_computation.4 | custom fusion | flops 262144 | bytes 3149824 | tf_op jit(solution)/shard_map/scatter-add | solution.py:66
  820.2 1.0 copy-done
  821.3 4.1 fusion.265
  827.0 305.0 %all-reduce.8.cloned.1.call-done = f32[2,128,1024]{1,0,2:T(2,128)} async-done(((f32[2,128,1024]{1,0,2:T(2,128)}), f32[2,128,1024]{1,0,2:T(2,128)}) %all-reduce.8.cloned.1.call-update) | async-done | bytes 1048592
  1133.5 36.9 %all-to-all-start = ((f32[2,128,32]{2,0,1:T(2,128)}), f32[2,128,32]{2,0,1:T(2,128)S(1)}, u32[]{:S(2)}, u32[]{:S(2)}) async-start(f32[2,128,32]{2,0,1:T(2,128)} %copy.424), calls=%async_computation.1 | async-start | bytes 262144 | tf_op jit(solution)/shard_map/all_to_all | solution.py:139
  1170.8 8.5 all-to-all-done
  1181.2 4.3 fusion
  1187.3 3.7 copy.433
  1191.0 5.4 all-to-all-start.3
  1196.3 3.6 copy.429
  1199.9 25.1 %all-to-all-done.3 = f32[2,1,4096]{0,1,2:T(1,128)S(1)} async-done(((f32[2,1,4096]{0,1,2:T(1,128)}), f32[2,1,4096]{0,1,2:T(1,128)S(1)}, u32[]{:S(2)}, u32[]{:S(2)}) %all-to-all-start.3) | async-done | bytes 32800 | tf_op jit(solution)/shard_map/all_to_all | solution.py:157
  1225.0 7.3 all-to-all-start.2
  1232.3 1.9 copy.436
  1234.3 26.5 %all-to-all-done.2 = f32[2,1,4096]{0,1,2:T(1,128)} async-done(((f32[2,1,4096]{0,1,2:T(1,128)}), f32[2,1,4096]{0,1,2:T(1,128)}, u32[]{:S(2)}, u32[]{:S(2)}) %all-to-all-start.2) | async-done | bytes 32800 | tf_op jit(solution)/shard_map/all_to_all | solution.py:150
  1260.8 3.3 copy.435
  (85 shorter events, 16.1 us)
Async XLA Ops:
  7.2 128.4 %all-gather.6.cloned.1.call-start = ((), (), s32[]{:S(2)}) async-start(), calls=%async_computation.7 | async-start | bytes 1081344 | tf_op jit(solution)/shard_map/all_gather | solution.py:127
  8.6 286.1 %reduce-scatter.2.cloned.1.call-start = ((), (), s32[]{:S(2)}) async-start(), calls=%async_computation.5 | async-start | bytes 540672 | tf_op jit(solution)/shard_map/reduce_scatter | solution.py:123
  17.3 591.6 %all-reduce.6.cloned.1.call-start = ((), (), s32[]{:S(2)}) async-start(), calls=%async_computation.8 | async-start | bytes 2097152
  138.5 10.1 copy-start.7
  155.9 38.9 %copy-start.5 = (s32[2]{0:T(128)S(1)}, s32[2]{0:T(128)}, u32[]{:S(2)}) copy-start(s32[2]{0:T(128)} %param.17) | copy-start | bytes 28
  156.0 40.8 %copy-start.8 = (u32[128]{0:T(128)S(1)}, u32[128]{0:T(128)}, u32[]{:S(2)}) copy-start(u32[128]{0:T(128)} %constant.117) | copy-start | bytes 1540
  156.0 453.6 %copy-start.2 = (f32[1,2,128,32]{2,3,1,0:T(8,128)S(1)}, f32[1,2,128,32]{2,3,1,0:T(8,128)}, u32[]{:S(2)}) copy-start(f32[1,2,128,32]{2,3,1,0:T(8,128)} %param.14) | copy-start | bytes 98308
  156.0 453.6 %copy-start.3 = (f32[1,2,128,32]{2,3,1,0:T(8,128)S(1)}, f32[1,2,128,32]{2,3,1,0:T(8,128)}, u32[]{:S(2)}) copy-start(f32[1,2,128,32]{2,3,1,0:T(8,128)} %param.9) | copy-start | bytes 98308
  156.0 453.6 %copy-start.4 = (f32[1,2,128,32]{2,3,1,0:T(8,128)S(1)}, f32[1,2,128,32]{2,3,1,0:T(8,128)}, u32[]{:S(2)}) copy-start(f32[1,2,128,32]{2,3,1,0:T(8,128)} %param.13) | copy-start | bytes 98308
  193.7 1.0 copy-start.1
  194.8 567.6 %all-gather.4.cloned.1.call-start = ((), (), s32[]{:S(2)}) async-start(), calls=%async_computation.6 | async-start | bytes 1081344 | tf_op jit(solution)/shard_map/all_gather | solution.py:127
  611.1 215.9 %all-to-all-start.1 = ((f32[2,128,32]{2,0,1:T(2,128)}), f32[2,128,32]{2,0,1:T(2,128)S(1)}, u32[]{:S(2)}, u32[]{:S(2)}) async-start(f32[2,128,32]{2,0,1:T(2,128)} %copy.426), calls=%async_computation.2 | async-start | bytes 262144 | tf_op jit(solution)/shard_map/all_to_all | solution.py:140
  647.6 484.4 %all-reduce.8.cloned.1.call-start = ((), (), s32[]{:S(2)}) async-start(), calls=%async_computation.9 | async-start | bytes 2097152
  782.5 38.8 %copy-start.6 = (s32[4]{0:T(128)S(1)}, s32[4]{0:T(128)}, u32[]{:S(2)}) copy-start(s32[4]{0:T(128)} %param.16) | copy-start | bytes 52
  820.2 1.0 copy-start
  1133.5 45.8 %all-to-all-start = ((f32[2,128,32]{2,0,1:T(2,128)}), f32[2,128,32]{2,0,1:T(2,128)S(1)}, u32[]{:S(2)}, u32[]{:S(2)}) async-start(f32[2,128,32]{2,0,1:T(2,128)} %copy.424), calls=%async_computation.1 | async-start | bytes 262144 | tf_op jit(solution)/shard_map/all_to_all | solution.py:139
  1191.0 34.1 %all-to-all-start.3 = ((f32[2,1,4096]{0,1,2:T(1,128)}), f32[2,1,4096]{0,1,2:T(1,128)S(1)}, u32[]{:S(2)}, u32[]{:S(2)}) async-start(f32[2,1,4096]{0,1,2:T(1,128)} %copy.433), calls=%async_computation.4 | async-start | bytes 4194304 | tf_op jit(solution)/shard_map/all_to_all | solution.py:157
  1225.0 35.7 %all-to-all-start.2 = ((f32[2,1,4096]{0,1,2:T(1,128)}), f32[2,1,4096]{0,1,2:T(1,128)}, u32[]{:S(2)}, u32[]{:S(2)}) async-start(f32[2,1,4096]{0,1,2:T(1,128)} %copy.429), calls=%async_computation.3 | async-start | bytes 4194304 | tf_op jit(solution)/shard_map/all_to_all | solution.py:150
Sparse Core Ops, SparseCore 0:
  10.2 125.3 all-gather.5
  137.9 156.8 reduce-scatter.1
  297.2 311.5 all-reduce.5
  610.9 151.3 all-gather.3
  821.4 310.5 all-reduce.7
where the time goes:
time: 1280 us; the launch traced here: 1270 us
  waiting for transfers between devices  1010 us (79%)
  starting transfers between devices  86.4 us (7%)
  other arithmetic  84.3 us (7%)
  local copies, waits for them, and re-layouts  39.4 us (3%)
  matrix products  37.5 us (3%)
  between operations  16.7 us (1%)
    unnamed x7, waiting for transfers between devices  618 us
    all_gather x2, waiting for transfers between devices, shards(): whole = lax.all_gather(strip, 'tile', axis=2, tiled=True)  231 us
    reduce_scatter x1, waiting for transfers between devices, shards(): lax.psum_scatter(illumination(starts, probe, total), 'tile', scatter_dime...  96.8 us
    scatter-add x2, other arithmetic, strip_gradient(): jnp.zeros((2, rows, total), jnp.float32).at[:, :, columns].add(values)  65.6 us
    all_to_all x1, starting transfers between devices, shards(): lax.all_to_all(strip, ('view', 'tile'), split_axis=1, concat_axis=2, tile...  36.9 us
    all_to_all x1, starting transfers between devices, shards(): lax.all_to_all(lagrange, ('view', 'tile'), split_axis=1, concat_axis=2, t...  36.6 us
    all_to_all x1, waiting for transfers between devices, shards(): lax.all_to_all(fresh.reshape(2, owned, views * total), ('view', 'tile'),...  26.5 us
  transfers between devices with their start and end apart: 9, of which 8 were waited for; matrix products, arithmetic and copies ran while one was open for 11% of the time, Pallas kernels for 0%

commit v1 on v0

v1 whole, which is shorter than its diff:
```python
import math

import jax
import jax.numpy as jnp
import ml_dtypes
import numpy as np
from jax import lax
from jax.experimental import pallas as pl
from jax.experimental.pallas import tpu as pltpu
from jax.sharding import PartitionSpec as P

ITERS = 2
F32 = jnp.float32
BF16 = jnp.bfloat16
MESH = pl.DeviceIdType.MESH

ROWS = 128
TOTAL = 1024
SCANS = 8
TILE = 32
FLOOR = 0.25 / math.sqrt(SCANS * 32 * ROWS // TOTAL)

PEERS = sorted(
    [(dz, dx) for dz in range(4) for dx in range(4) if (dz, dx) != (0, 0)],
    key=lambda p: -(min(p[0], 4 - p[0]) + min(p[1], 4 - p[1])),
)


def dft_matrices():
    idx = np.arange(ROWS)
    phase = (idx[:, None] * idx[None, :] % ROWS) * (2.0 * math.pi / ROWS)
    c = np.cos(phase) / math.sqrt(ROWS)
    s = -np.sin(phase) / math.sqrt(ROWS)
    out = []
    for m in (np.block([[c, s], [-s, c]]), np.block([[c, -s], [s, c]])):
        m = m.astype(np.float32)
        hi = m.astype(ml_dtypes.bfloat16)
        lo = (m - hi.astype(np.float32)).astype(ml_dtypes.bfloat16)
        out.append(np.stack([hi, lo]))
    return np.stack(out)


def split(x):
    hi = x.astype(BF16)
    return hi, (x - hi.astype(F32)).astype(BF16)


def split3(x):
    hi = x.astype(BF16)
    rest = x - hi.astype(F32)
    mid = rest.astype(BF16)
    return hi, mid, (rest - mid.astype(F32)).astype(BF16)


def dot(a, b):
    return jnp.dot(a, b, preferred_element_type=F32)


def dot_nt(a, b):
    return lax.dot_general(a, b, (((1,), (1,)), ((), ())), preferred_element_type=F32)


def dot_tn(a, b):
    return lax.dot_general(a, b, (((0,), (0,)), ((), ())), preferred_element_type=F32)


def dot3(a, b):
    return dot(a[0], b[0]) + (dot(a[1], b[0]) + dot(a[0], b[1]))


def device(z, y, x, k):
    return ((y // 2) * 2 + k, z * 8 + (y % 2) * 4 + x)


def kernel(
    pos_s, ang_s, pen_s, obj_h, probe_h, amp_h, prev_h, mult_h, vol_h, mat_h,
    fresh_o, renew_o,
    strip1, strip2, acc1, acc2, zbuf, sharein1, sharein2, stage1, stage2, rsin1, rsin2,
    amp_r, amp_t, probe_v, probe_t, prev_r, mult_r, vol_v, mat_v,
    posb, posr, posall, posm, sums, flips, lbuf, mbuf, nbuf, qbuf, qmat, wfull, vec, qmsg, qflip, qall,
    sem_swap, sem_swap_send, sem_loc, sem_vol, sem_ag_s, sem_ag, sem_sh_s, sem_sh, sem_acc_s, sem_acc,
    sem_rs_s, sem_rs, sem_ln_s, sem_ln, sem_ps_s, sem_ps, sem_q_s, sem_q, sem_smem,
):
    view = lax.axis_index("view")
    tile = lax.axis_index("tile")
    yh, k = view // 2, view % 2
    z, yl, x = tile // 8, (tile // 4) % 2, tile % 4
    y = yh * 2 + yl
    role = z * 8 + k * 4 + x
    own = pl.multiple_of(role * TILE, TILE)
    given = pl.multiple_of(tile * TILE, TILE)
    swapped = yl != k
    partner = device(z, yh * 2 + k, x, yl)
    twin = device(z, y, x, 1 - k)
    fours = range(4)

    def local(src, dst, sem):
        return pltpu.make_async_copy(src, dst, sem)

    def remote(src, dst, send, recv, to):
        return pltpu.make_async_remote_copy(
            src_ref=src, dst_ref=dst, send_sem=send, recv_sem=recv, device_id=to, device_id_type=MESH
        )

    def drain(ref, sem):
        pltpu.make_async_copy(ref, ref, sem).wait()

    def peer(dz, dx):
        return device((z + dz) % 4, y, (x + dx) % 4, k)

    loc = [local(probe_h, probe_v, sem_loc.at[0]), local(mat_h, mat_v, sem_loc.at[1])]
    vols = [
        local(vol_h.at[comp, pl.ds(256 * q, 256)], vol_v.at[comp, pl.ds(256 * q, 256)], sem_vol.at[comp * 4 + q])
        for comp in range(2)
        for q in fours
    ]
    for copy in loc + vols:
        copy.start()

    barrier = pltpu.get_barrier_semaphore()
    greeted = 0
    for dz, dx in PEERS:
        pl.semaphore_signal(barrier, inc=1, device_id=peer(dz, dx), device_id_type=MESH)
        greeted += 1
    for dy in fours:
        for dk in range(2):
            if (dy, dk) != (0, 0):
                pl.semaphore_signal(
                    barrier, inc=1, device_id=device(z, (y + dy) % 4, x, (k + dk) % 2), device_id_type=MESH
                )
                pl.semaphore_signal(
                    barrier, inc=1, device_id=device(3 - z, (y + dy) % 4, 3 - x, (k + dk) % 2), device_id_type=MESH
                )
                greeted += 2
    for p in range(SCANS):
        posb[p : p + 1, :] = jnp.full((1, 128), pos_s[0, p], jnp.int32)
    zeros = jnp.zeros((128, 128), F32)
    for s in range(SCANS):
        for comp in range(2):
            zbuf[s, comp, 0:128] = zeros
            zbuf[s, comp, 256:384] = zeros
    pl.semaphore_wait(barrier, greeted)

    trades = [
        (obj_h, strip1.at[:, pl.ds(given, TILE)], strip1.at[:, pl.ds(own, TILE)]),
        (posb, posr, posr),
        (prev_h, prev_r, prev_r),
        (mult_h, mult_r, mult_r),
        (amp_h, amp_r, amp_r),
    ]

    @pl.when(swapped)
    def _():
        for i, (src, dst, _) in enumerate(trades):
            remote(src, dst, sem_swap_send.at[i], sem_swap.at[i], partner).start()

    @pl.when(jnp.logical_not(swapped))
    def _():
        for i, (src, _, dst) in enumerate(trades):
            local(src, dst, sem_swap.at[i]).start()

    def traded(i):
        drain(trades[i][2], sem_swap.at[i])

    ones8 = jnp.ones((8, 128), BF16)

    def volume_sums(comp):
        col = jnp.zeros((8, 1024), F32)
        for q in fours:
            vols[comp * 4 + q].wait()
            for half in range(2):
                def body(i, carry):
                    col, part = carry
                    base = pl.multiple_of(256 * q + 128 * half + 8 * i, 8)
                    v = vol_v[comp, pl.ds(base, 8), :]
                    r = v[:, 0:128]
                    for j in range(1, 8):
                        r = r + v[:, 128 * j : 128 * j + 128]
                    qmat[pl.ds(pl.multiple_of(8 * i, 8), 8), :] = r
                    return col + v, part

                col, _ = lax.fori_loop(0, 16, body, (col, 0), unroll=4)
                parts = split3(qmat[...])
                line = dot_nt(ones8, parts[0]) + (dot_nt(ones8, parts[1]) + dot_nt(ones8, parts[2]))
                b = 2 * q + half
                sums[2 * comp + 1, b : b + 1, :] = line[0:1]
        for b in range(8):
            sums[2 * comp, b : b + 1, :] = jnp.sum(col[:, 128 * b : 128 * b + 128], axis=0, keepdims=True)

    volume_sums(0)

    def gather_start(strip, n):
        mine = strip.at[:, pl.ds(own, TILE)]
        for j, (dz, dx) in enumerate(PEERS):
            remote(mine, mine, sem_ag_s.at[n], sem_ag.at[n, j], peer(dz, dx)).start()
        remote(mine, mine, sem_sh_s.at[n], sem_sh.at[n], twin).start()

    def gather_finish(strip, n):
        for j in reversed(range(15)):
            dz, dx = PEERS[j]
            src = (z - dz + 4) % 4 * 8 + k * 4 + (x - dx + 4) % 4
            part = strip.at[:, pl.ds(pl.multiple_of(src * TILE, TILE), TILE)]
            drain(part, sem_ag.at[n, j])
            remote(part, part, sem_sh_s.at[n], sem_sh.at[n], twin).start()
        drain(strip.at[0], sem_sh.at[n])

    traded(0)
    gather_start(strip1, 0)

    traded(1)
    to_smem = local(posr, posm, sem_smem)
    to_smem.start()
    local(posr, posall.at[k, z, x], sem_ps.at[6]).start()
    for d in range(1, 4):
        remote(posr, posall.at[k, z, x], sem_ps_s.at[d - 1], sem_ps.at[d - 1], peer(0, d)).start()

    volume_sums(1)

    flat = sums[...].reshape(32, 128)
    rr = lax.broadcasted_iota(jnp.int32, (128, 128), 0)
    cc = lax.broadcasted_iota(jnp.int32, (128, 128), 1)
    anti = jnp.where(rr + cc == 127, 1.0, 0.0).astype(BF16)
    parts = split3(flat)
    turned = dot(parts[0], anti) + (dot(parts[1], anti) + dot(parts[2], anti))
    for a in fours:
        for b in range(8):
            flips[a, 7 - b : 8 - b, :] = turned[8 * a + b : 8 * a + b + 1]
    lane = lax.broadcasted_iota(jnp.int32, (8, 128), 1)
    scale = 1.0 / math.sqrt(TOTAL)
    whole = [jnp.sum(jnp.sum(sums[2 * c], axis=1, keepdims=True), axis=0, keepdims=True) * scale for c in range(2)]
    for u in fours:
        angle = ang_s[u]
        lines = []
        for c in range(2):
            lines.append(
                jnp.where(
                    angle == 0,
                    sums[2 * c],
                    jnp.where(angle == 1, sums[2 * c + 1], jnp.where(angle == 2, flips[2 * c], flips[2 * c + 1])),
                )
                * scale
            )
        for j in fours:
            re = lines[0] if j == 0 else pltpu.roll(lines[0], 128 - 32 * j, 1)
            im = lines[1] if j == 1 else pltpu.roll(lines[1], (160 - 32 * j) % 128, 1)
            rows = jnp.where(
                lane < 32,
                re,
                jnp.where(lane < 64, im, jnp.where(lane == 64, whole[0], whole[1])),
            )
            for b in range(8):
                e = (u // 2 * 2 + b % 2) * 2 + u % 2
                lbuf[j, b // 2, e] = rows[b : b + 1]
    local(lbuf.at[x], mbuf.at[x], sem_ln.at[0, 3]).start()
    for d in range(1, 4):
        xd = (x + d) % 4
        remote(lbuf.at[xd], mbuf.at[x], sem_ln_s.at[0, d - 1], sem_ln.at[0, d - 1], peer(0, d)).start()

    for copy in loc:
        copy.wait()
    for comp in range(2):
        probe_t[comp] = probe_v[comp].T
    to_smem.wait()

    gather_finish(strip1, 0)

    for d in range(1, 4):
        drain(posr, sem_ps.at[d - 1])
    drain(posr, sem_ps.at[6])
    for d in range(1, 4):
        remote(posall.at[k, z], posall.at[k, z], sem_ps_s.at[2 + d], sem_ps.at[2 + d], peer(d, 0)).start()

    pr, pi = probe_t[0], probe_t[1]

    traded(4)
    for s in range(SCANS):
        amp_t[s // 2, :, (s % 2) * 128 : (s % 2) * 128 + 128] = amp_r[s].T

    def compute(strip):
        forward = (mat_v[0, 0], mat_v[0, 1])
        inverse = (mat_v[1, 0], mat_v[1, 1])
        pr, pi = probe_t[0], probe_t[1]

        def pair(p, carry):
            exits = []
            for i in range(2):
                start = posm[2 * p + i, 0]
                wr = strip[0, pl.ds(start, 128), :]
                wi = strip[1, pl.ds(start, 128), :]
                exits.append(jnp.concatenate([pr * wr - pi * wi, pr * wi + pi * wr], axis=1))
            a = dot3(split(jnp.concatenate(exits, axis=0)), forward)
            a = jnp.concatenate(
                [
                    jnp.concatenate([a[:128, :128], a[128:, :128]], axis=1),
                    jnp.concatenate([a[:128, 128:], a[128:, 128:]], axis=1),
                ],
                axis=0,
            )
            f = dot3(inverse, split(a))
            fr, fi = f[:128], f[128:]
            g = amp_t[p] * lax.rsqrt(jnp.maximum(fr * fr + fi * fi, FLOOR * FLOOR))
            h = dot3(forward, split(jnp.concatenate([fr * g, fi * g], axis=0)))
            h = jnp.concatenate(
                [
                    jnp.concatenate([h[:128, :128], h[128:, :128]], axis=1),
                    jnp.concatenate([h[:128, 128:], h[128:, 128:]], axis=1),
                ],
                axis=0,
            )
            b = dot3(split(h), inverse)
            for i in range(2):
                br, bi = b[128 * i : 128 * i + 128, :128], b[128 * i : 128 * i + 128, 128:]
                zbuf[2 * p + i, 0, 128:256] = pr * br + pi * bi
                zbuf[2 * p + i, 1, 128:256] = pr * bi - pi * br
            return carry

        lax.fori_loop(0, SCANS // 2, pair, 0)

    def own_weight():
        return wfull[role // 4, pl.ds(pl.multiple_of(role % 4 * 32, 32), 32), :]

    def block_sum(comp, b):
        total = None
        for s in range(SCANS):
            off = jnp.clip(128 + 128 * b - posm[s, 0], 0, 256)
            part = zbuf[s, comp, pl.ds(off, 128), :]
            total = part if total is None else total + part
        return total

    def scatter_start(acc, sharein, stage, n, rho, messages):
        height = stage.shape[2]
        if messages:
            vec[...] = jnp.zeros((8, 128), F32)
            for comp in range(2):
                extra = mult_r[comp] / rho + (rho * prev_r[comp] - mult_r[comp]) * own_weight()
                vec[comp : comp + 1, :] = jnp.sum(extra, axis=0, keepdims=True)
        for which in (1 - k, k):
            def body(j, carry, which=which):
                b = 2 * j + which
                for comp in range(2):
                    total = block_sum(comp, b)
                    acc[which, j, comp] = total
                    if messages:
                        vec[comp : comp + 1, :] += jnp.sum(total * wfull[b], axis=0, keepdims=True)
                return carry
            for j in fours:
                body(j, 0)
                if which is not k:
                    remote(acc.at[which, j], sharein.at[j], sem_acc_s.at[n], sem_acc.at[n, j], twin).start()
        for i in fours:
            zd = (z + (2, 1, 3, 0)[i]) % 4
            drain(sharein.at[zd], sem_acc.at[n, zd])
            for xd in fours:
                for comp in range(2):
                    rows = slice(32 * xd, 32 * xd + 32)
                    stage[zd, xd, 32 * comp : 32 * comp + 32] = acc[k, zd, comp, rows] + sharein[zd, comp, rows]
                if messages:
                    stage[zd, xd, 64:72] = vec[...]
            dz = (2, 1, 3, 0)[i]
            if dz == 0:
                for comp in range(2):
                    rows = slice(32 * comp, 32 * comp + 32)
                    stage[z, x, rows] = stage[z, x, rows] + (rho * prev_r[comp] - mult_r[comp])
            for dx in (2, 1, 3, 0):
                if (dz, dx) != (0, 0):
                    j = PEERS.index((dz, dx))
                    remote(
                        stage.at[zd, (x + dx) % 4], scatter_in[n].at[j], sem_rs_s.at[n], sem_rs.at[n], peer(dz, dx),
                    ).start()

    scatter_in = (rsin1, rsin2)

    def scatter_finish(stage, n):
        drain(scatter_in[n].at[pl.ds(0, 15)], sem_rs.at[n])
        total = stage[z, x]
        for j in range(15):
            total = total + scatter_in[n][j]
        return total

    rho = jnp.full((32, 128), pen_s[0], jnp.int32).astype(F32) / jnp.full((32, 128), pen_s[1], jnp.int32).astype(F32)

    compute(strip1)
    traded(2)
    traded(3)
    scatter_start(acc1, sharein1, stage1, 0, rho, False)

    for d in range(1, 4):
        drain(posall.at[k, z], sem_ps.at[2 + d])
    remote(posall.at[k], posall.at[k], sem_ps_s.at[6], sem_ps.at[7], twin).start()
    for d in range(4):
        drain(mbuf.at[0], sem_ln.at[0, d])
    local(mbuf.at[:, z], nbuf.at[z], sem_ln.at[1, 3]).start()
    for d in range(1, 4):
        zd = (z + d) % 4
        remote(mbuf.at[:, zd], nbuf.at[z], sem_ln_s.at[1, d - 1], sem_ln.at[1, d - 1], peer(d, 0)).start()

    drain(posall.at[0], sem_ps.at[7])
    where = posall[...].reshape(256, 128)
    lanes = lax.broadcasted_iota(jnp.int32, (256, 128), 1)
    high = jnp.where(lanes == (where >> 7), 1.0, 0.0)
    low = jnp.where(lanes == ((128 - (where & 127)) & 127), 1.0, 0.0)
    counts = dot_tn(high.astype(BF16), low.astype(BF16))
    power = split(pr * pr + pi * pi)
    before = jnp.zeros((128, 128), F32)
    for b in range(8):
        here = pltpu.roll(jnp.broadcast_to(counts[b : b + 1], (128, 128)), 0, 1, stride=1, stride_axis=0)
        toeplitz = jnp.where(rr >= cc, here, before).astype(BF16)
        before = here
        wfull[b] = 1.0 / (dot(toeplitz, power[0]) + dot(toeplitz, power[1]) + rho[0:1])
    weight = own_weight()

    total = scatter_finish(stage1, 0)
    for comp in range(2):
        strip2[comp, pl.ds(own, TILE), :] = total[32 * comp : 32 * comp + 32] * weight
    gather_start(strip2, 1)
    for d in range(4):
        drain(nbuf.at[0], sem_ln.at[1, d])
    e = y * 2 + k
    local(nbuf.at[:, :, e], qbuf.at[yh * 2 + k, :, yl], sem_ln.at[2, 7]).start()
    i = 0
    for dy in fours:
        for dk in range(2):
            if (dy, dk) != (0, 0):
                yd, kd = (y + dy) % 4, (k + dk) % 2
                remote(
                    nbuf.at[:, :, yd * 2 + kd], qbuf.at[yh * 2 + k, :, yl],
                    sem_ln_s.at[2, i], sem_ln.at[2, i], device(z, yd, x, kd),
                ).start()
                i += 1
    gather_finish(strip2, 1)

    compute(strip2)
    scatter_start(acc2, sharein2, stage2, 1, rho, True)

    for d in range(8):
        drain(nbuf.at[:, :, 0], sem_ln.at[2, d])
    for h in range(128):
        qmat[h : h + 1, :] = qbuf[h // 32, h // 8 % 4, h // 4 % 2, h % 4]
    lines = qmat[...].T

    total = scatter_finish(stage2, 1)
    for comp in range(2):
        rows = slice(32 * comp, 32 * comp + 32)
        qmsg[rows] = total[rows] * weight + mult_r[comp] / rho
    qmsg[64:72] = total[64:72]
    for comp in range(2):
        for i in range(32):
            qflip[32 * comp + 31 - i : 32 * comp + 32 - i] = qmsg[32 * comp + i : 32 * comp + i + 1]
    qflip[64:72] = total[64:72]
    for u in fours:
        to = device(3 - z, u // 2 * 2 + 1 - k, 3 - x, u % 2)
        remote(qflip, qall.at[4 + y], sem_q_s.at[0], sem_q, to).start()
    for i in range(3):
        d = i + 1
        yd, kd = ((yh + d // 2) % 2) * 2 + k, (k + d % 2) % 2
        remote(qmsg, qall.at[y], sem_q_s.at[1], sem_q, device(z, yd, x, kd)).start()

    @pl.when(swapped)
    def _():
        remote(qmsg, qall.at[y], sem_q_s.at[2], sem_q, device(z, yh * 2 + k, x, k)).start()

    @pl.when(jnp.logical_not(swapped))
    def _():
        local(qmsg, qall.at[y], sem_q).start()

    drain(qall, sem_q)
    qs, qm = qall.at[pl.ds(0, 4)], qall.at[pl.ds(4, 4)]

    mine = ang_s[yh * 2 + k]
    same = [jnp.where(ang_s[u] == mine, 1.0, 0.0) for u in fours]
    turned = [jnp.where(ang_s[u] == lax.rem(mine + 2, 4), 1.0, 0.0) for u in fours]
    other = [1.0 - same[u] - turned[u] for u in fours]
    members = same[0] + same[1] + same[2] + same[3] + turned[0] + turned[1] + turned[2] + turned[3]
    for comp in range(2):
        rows = slice(32 * comp, 32 * comp + 32)
        line = lines[rows]
        spread = (4.0 - members) * lines[64 + comp : 65 + comp]
        mix = members * line
        for u in fours:
            mix = mix - same[u] * qs[u, rows] - turned[u] * qm[u, rows]
            spread = spread - other[u] * (qs[u, 64 + comp : 65 + comp] + qm[u, 64 + comp : 65 + comp])
        fresh = line - 0.25 * (mix + spread * (1.0 / TOTAL))
        fresh_o[comp] = fresh
        keep = jnp.zeros((32, 128), F32)
        for u in fours:
            keep = keep + jnp.where(yh * 2 + k == u, qs[u, rows], 0.0)
        renew_o[comp] = rho * (keep - fresh)

    @pl.when(swapped)
    def _():
        for i, (src, _, dst) in enumerate(trades):
            drain(dst, sem_swap_send.at[i])
        drain(qmsg, sem_q_s.at[2])

    drain(qs, sem_q_s.at[0])
    drain(qs.at[pl.ds(0, 3)], sem_q_s.at[1])
    for n, strip in ((0, strip1), (1, strip2)):
        drain(strip.at[0, pl.ds(0, 960)], sem_ag_s.at[n])
        drain(strip.at[0], sem_sh_s.at[n])
        drain(scatter_in[n].at[pl.ds(0, 15)], sem_rs_s.at[n])
        drain((sharein1, sharein2)[n], sem_acc_s.at[n])
    for d in range(3):
        drain(posr, sem_ps_s.at[d])
        drain(posall.at[k, z], sem_ps_s.at[3 + d])
        drain(lbuf.at[0], sem_ln_s.at[0, d])
        drain(nbuf.at[0], sem_ln_s.at[1, d])
    drain(posall.at[0], sem_ps_s.at[6])
    for d in range(7):
        drain(nbuf.at[:, :, 0], sem_ln_s.at[2, d])


def shards(objects, probe, positions, amplitudes, reproj_prev, multipliers, volume, angles, penalty):
    across = lambda a: jnp.transpose(a[0], (0, 2, 1))
    any_, vmem, smem = (pl.BlockSpec(memory_space=m) for m in (pl.ANY, pltpu.VMEM, pltpu.SMEM))
    mats = jnp.asarray(dft_matrices())
    dma = pltpu.SemaphoreType.DMA
    out = jax.ShapeDtypeStruct((2, TILE, ROWS), F32)
    scratch = [
        pltpu.VMEM((2, TOTAL, ROWS), F32),
        pltpu.VMEM((2, TOTAL, ROWS), F32),
        pltpu.VMEM((2, 4, 2, 128, 128), F32),
        pltpu.VMEM((2, 4, 2, 128, 128), F32),
        pltpu.VMEM((SCANS, 2, 384, 128), F32),
        pltpu.VMEM((4, 2, 128, 128), F32),
        pltpu.VMEM((4, 2, 128, 128), F32),
        pltpu.VMEM((4, 4, 64, 128), F32),
        pltpu.VMEM((4, 4, 72, 128), F32),
        pltpu.VMEM((16, 64, 128), F32),
        pltpu.VMEM((16, 72, 128), F32),
        pltpu.VMEM((SCANS, 128, 128), F32),
        pltpu.VMEM((SCANS // 2, 128, 256), F32),
        pltpu.VMEM((2, 128, 128), F32),
        pltpu.VMEM((2, 128, 128), F32),
        pltpu.VMEM((2, TILE, ROWS), F32),
        pltpu.VMEM((2, TILE, ROWS), F32),
        pltpu.VMEM((2, TOTAL, TOTAL), F32),
        pltpu.VMEM((2, 2, 256, 256), BF16),
        pltpu.VMEM((SCANS, 128), jnp.int32),
        pltpu.VMEM((SCANS, 128), jnp.int32),
        pltpu.VMEM((2, 4, 4, SCANS, 128), jnp.int32),
        pltpu.SMEM((SCANS, 128), jnp.int32),
        pltpu.VMEM((4, 8, 128), F32),
        pltpu.VMEM((4, 8, 128), F32),
        pltpu.VMEM((4, 4, 8, 1, 128), F32),
        pltpu.VMEM((4, 4, 8, 1, 128), F32),
        pltpu.VMEM((4, 4, 8, 1, 128), F32),
        pltpu.VMEM((4, 4, 2, 4, 1, 128), F32),
        pltpu.VMEM((128, 128), F32),
        pltpu.VMEM((8, 128, 128), F32),
        pltpu.VMEM((8, 128), F32),
        pltpu.VMEM((72, 128), F32),
        pltpu.VMEM((72, 128), F32),
        pltpu.VMEM((8, 72, 128), F32),
        dma((5,)), dma((5,)), dma((2,)), dma((8,)),
        dma((2,)), dma((2, 15)), dma((2,)), dma((2,)),
        dma((2,)), dma((2, 4)), dma((2,)), dma((2,)),
        dma((3, 8)), dma((3, 8)), dma((8,)), dma((8,)),
        dma((3,)), dma, dma,
    ]
    fresh, renewed = pl.pallas_call(
        kernel,
        out_shape=(out, out),
        in_specs=[smem, smem, smem] + [any_] * 7,
        out_specs=(vmem, vmem),
        scratch_shapes=scratch,
        compiler_params=pltpu.CompilerParams(
            collective_id=0, has_side_effects=True, vmem_limit_bytes=60 * 1024 * 1024
        ),
    )(
        positions,
        angles,
        penalty,
        across(objects),
        probe,
        amplitudes[0],
        across(reproj_prev),
        across(multipliers),
        volume[:, 0],
        mats,
    )
    back = lambda a: jnp.transpose(a, (0, 2, 1))[None]
    return back(fresh), back(renewed)


def solution(mesh):
    return jax.shard_map(
        shards,
        mesh=mesh,
        in_specs=(
            P("view", None, None, "tile"),
            P(),
            P("view", "tile"),
            P("view", "tile", None, None),
            P("view", None, None, "tile"),
            P("view", None, None, "tile"),
            P(None, ("view", "tile"), None, None),
            P(),
            P(),
        ),
        out_specs=(P("view", None, None, "tile"), P("view", None, None, "tile")),
        check_vma=False,
    )
```

time: 1280 us -> 74.7 us (0.06)
  waiting for transfers between devices: 1010 us -> 0 us
  starting transfers between devices: 86.4 us -> 0 us
  other arithmetic: 84.3 us -> 0 us
  Pallas kernels: 0 us -> 69.9 us
  matrix products: 37.5 us -> 0 us
  local copies, waits for them, and re-layouts: 39.4 us -> 2.75 us
  between operations: 16.7 us -> 0.64 us
    unnamed x7 -> x0, waiting for transfers between devices: 618 us -> none
    all_gather x2 -> x0, waiting for transfers between devices: 231 us -> none  [shards(): whole = lax.all_gather(strip, 'tile', axis=2, tiled=True)]
    reduce_scatter x1 -> x0, waiting for transfers between devices: 96.8 us -> none  [shards(): lax.psum_scatter(illumination(starts, probe, total), 'tile', scatter_dime...]
    all_to_all x4 -> x0, starting transfers between devices: 86.1 us -> none  [the longest x1 36.9 us: shards(): lax.all_to_all(strip, ('view', 'tile'), split_axis=1, concat_axis=2, tile...]
    scatter-add x3 -> x0, other arithmetic: 72.4 us -> none  [the longest x2 65.6 us: strip_gradient(): jnp.zeros((2, rows, total), jnp.float32).at[:, :, columns].add(values)]
    pallas_call x0 -> x1, Pallas kernels: none -> 69.9 us  [shards(): pl.pallas_call(kernel, out_shape=(out, out), in_specs=[smem, smem, smem]...]
    all_to_all x4 -> x0, waiting for transfers between devices: 60.1 us -> none  [the longest x1 26.5 us: shards(): lax.all_to_all(fresh.reshape(2, owned, views * total), ('view', 'tile'),...]
    dot_general x32 -> x0, matrix products: 37.5 us -> none  [the longest x4 5.26 us: left_apply(): first = jnp.einsum('rk,nkc->nrc', cosine, real_part, precision=HIGHEST)]
  transfers between devices with their start and end apart: 9 -> 0, of which waited for: 8 -> 0; matrix products, arithmetic and copies ran while one was open for 11% -> 0% of each run, Pallas kernels for 0% -> 0%
where the time goes in v1:
time: 74.7 us; the launch traced here: 73.3 us
  Pallas kernels  69.9 us (94%)
  local copies, waits for them, and re-layouts  2.75 us (4%)
    pallas_call x1, Pallas kernels, shards(): pl.pallas_call(kernel, out_shape=(out, out), in_specs=[smem, smem, smem]...  69.9 us
    unnamed x2, local copies, waits for them, and re-layouts  2.75 us

profile of v1, /device:TPU:9, one launch (start us, length us, event | category | flops | bytes accessed | tf_op | source)
XLA Modules:
  0.0 73.3 jit_solution(15876989211770187288)
XLA Ops:
  0.6 69.9 %shard_map.113 = (f32[2,32,128]{2,1,0:T(8,128)}, f32[2,32,128]{2,1,0:T(8,128)}) custom-call(s32[1,8]{1,0:T(1,128)} %pos_s.1, s32[4]{0:T(128)} %ang_s.1, s32[2]{0:T(128)} %pen_s.1, f32[2,32,128]{2,1,0:T(8,128)} %bitcast.19, f32[2,128,128]{2,1,0:T(8,128)} %probe_h.1, f32[8,128,128]{2,1,0:T(8,128)} %bitcast.18, f32[2,32,128]{2,1,0:T(8,128)} %bitcast.20, ...), custom_call_target="tpu_custom_call" | custom-call | tf_op jit(solution)/shard_map/pallas_call | solution.py:560
  70.5 1.4 %copy.14 = f32[1,2,128,32]{2,3,1,0:T(8,128)} copy(f32[1,2,128,32]{2,3,1,0:T(8,128)} %bitcast.23) | data formatting | bytes 65536
  71.9 1.4 %copy.15 = f32[1,2,128,32]{2,3,1,0:T(8,128)} copy(f32[1,2,128,32]{2,3,1,0:T(8,128)} %bitcast.22) | data formatting | bytes 65536

commit v2 on v1

--- a/solution.py
+++ b/solution.py
@@ -149,15 +149,19 @@
         (amp_h, amp_r, amp_r),
     ]
 
-    @pl.when(swapped)
-    def _():
-        for i, (src, dst, _) in enumerate(trades):
-            remote(src, dst, sem_swap_send.at[i], sem_swap.at[i], partner).start()
-
-    @pl.when(jnp.logical_not(swapped))
-    def _():
-        for i, (src, _, dst) in enumerate(trades):
-            local(src, dst, sem_swap.at[i]).start()
+    def start_trade(i):
+        src, there, here = trades[i]
+
+        @pl.when(swapped)
+        def _():
+            remote(src, there, sem_swap_send.at[i], sem_swap.at[i], partner).start()
+
+        @pl.when(jnp.logical_not(swapped))
+        def _():
+            local(src, here, sem_swap.at[i]).start()
+
+    for i in range(4):
+        start_trade(i)
 
     def traded(i):
         drain(trades[i][2], sem_swap.at[i])
@@ -189,23 +193,26 @@
 
     volume_sums(0)
 
-    def gather_start(strip, n):
-        mine = strip.at[:, pl.ds(own, TILE)]
+    def gather_start(strip, n, comp):
+        mine = strip.at[comp, pl.ds(own, TILE)]
         for j, (dz, dx) in enumerate(PEERS):
-            remote(mine, mine, sem_ag_s.at[n], sem_ag.at[n, j], peer(dz, dx)).start()
+            remote(mine, mine, sem_ag_s.at[n], sem_ag.at[n, comp, j], peer(dz, dx)).start()
         remote(mine, mine, sem_sh_s.at[n], sem_sh.at[n], twin).start()
 
     def gather_finish(strip, n):
-        for j in reversed(range(15)):
-            dz, dx = PEERS[j]
-            src = (z - dz + 4) % 4 * 8 + k * 4 + (x - dx + 4) % 4
-            part = strip.at[:, pl.ds(pl.multiple_of(src * TILE, TILE), TILE)]
-            drain(part, sem_ag.at[n, j])
-            remote(part, part, sem_sh_s.at[n], sem_sh.at[n], twin).start()
+        for comp in range(2):
+            for j in reversed(range(15)):
+                dz, dx = PEERS[j]
+                src = (z - dz + 4) % 4 * 8 + k * 4 + (x - dx + 4) % 4
+                part = strip.at[comp, pl.ds(pl.multiple_of(src * TILE, TILE), TILE)]
+                drain(part, sem_ag.at[n, comp, j])
+                remote(part, part, sem_sh_s.at[n], sem_sh.at[n], twin).start()
         drain(strip.at[0], sem_sh.at[n])
 
     traded(0)
-    gather_start(strip1, 0)
+    for comp in range(2):
+        gather_start(strip1, 0, comp)
+    start_trade(4)
 
     traded(1)
     to_smem = local(posr, posm, sem_smem)
@@ -314,7 +321,7 @@
                 zbuf[2 * p + i, 1, 128:256] = pr * bi - pi * br
             return carry
 
-        lax.fori_loop(0, SCANS // 2, pair, 0)
+        lax.fori_loop(0, SCANS // 2, pair, 0, unroll=True)
 
     def own_weight():
         return wfull[role // 4, pl.ds(pl.multiple_of(role % 4 * 32, 32), 32), :]
@@ -327,54 +334,54 @@
             total = part if total is None else total + part
         return total
 
-    def scatter_start(acc, sharein, stage, n, rho, messages):
-        height = stage.shape[2]
-        if messages:
+    def scatter_start(acc, sharein, stage, n, rho):
+        if n:
             vec[...] = jnp.zeros((8, 128), F32)
             for comp in range(2):
                 extra = mult_r[comp] / rho + (rho * prev_r[comp] - mult_r[comp]) * own_weight()
                 vec[comp : comp + 1, :] = jnp.sum(extra, axis=0, keepdims=True)
-        for which in (1 - k, k):
-            def body(j, carry, which=which):
-                b = 2 * j + which
-                for comp in range(2):
-                    total = block_sum(comp, b)
-                    acc[which, j, comp] = total
-                    if messages:
-                        vec[comp : comp + 1, :] += jnp.sum(total * wfull[b], axis=0, keepdims=True)
-                return carry
+
+        def blocks(comp, parity):
             for j in fours:
-                body(j, 0)
-                if which is not k:
-                    remote(acc.at[which, j], sharein.at[j], sem_acc_s.at[n], sem_acc.at[n, j], twin).start()
-        for i in fours:
-            zd = (z + (2, 1, 3, 0)[i]) % 4
-            drain(sharein.at[zd], sem_acc.at[n, zd])
-            for xd in fours:
-                for comp in range(2):
+                i = 2 * j + parity
+                total = block_sum(comp, i)
+                acc[parity, comp, j] = total
+                if n:
+                    vec[comp : comp + 1, :] += jnp.sum(total * wfull[i], axis=0, keepdims=True)
+
+        for comp in range(2):
+            blocks(comp, 1 - k)
+            remote(acc.at[1 - k, comp], sharein.at[comp], sem_acc_s.at[n], sem_acc.at[n, comp], twin).start()
+        for comp in range(2):
+            blocks(comp, k)
+            drain(sharein.at[comp], sem_acc.at[n, comp])
+            for zd in fours:
+                for xd in fours:
                     rows = slice(32 * xd, 32 * xd + 32)
-                    stage[zd, xd, 32 * comp : 32 * comp + 32] = acc[k, zd, comp, rows] + sharein[zd, comp, rows]
-                if messages:
-                    stage[zd, xd, 64:72] = vec[...]
-            dz = (2, 1, 3, 0)[i]
-            if dz == 0:
-                for comp in range(2):
-                    rows = slice(32 * comp, 32 * comp + 32)
-                    stage[z, x, rows] = stage[z, x, rows] + (rho * prev_r[comp] - mult_r[comp])
-            for dx in (2, 1, 3, 0):
-                if (dz, dx) != (0, 0):
-                    j = PEERS.index((dz, dx))
-                    remote(
-                        stage.at[zd, (x + dx) % 4], scatter_in[n].at[j], sem_rs_s.at[n], sem_rs.at[n], peer(dz, dx),
-                    ).start()
+                    stage[comp, zd, xd, 0:32] = acc[k, comp, zd, rows] + sharein[comp, zd, rows]
+                    if n and comp:
+                        stage[comp, zd, xd, 32:40] = vec[...]
+            mine = pl.ds(0, 32)
+            stage[comp, z, x, mine] = stage[comp, z, x, mine] + (rho * prev_r[comp] - mult_r[comp])
+            height = 40 if n and comp else 32
+            for j, (dz, dx) in enumerate(PEERS):
+                remote(
+                    stage.at[comp, (z + dz) % 4, (x + dx) % 4, pl.ds(0, height)],
+                    scatter_in[n].at[comp, j, pl.ds(0, height)],
+                    sem_rs_s.at[n, comp], sem_rs.at[n, comp], peer(dz, dx),
+                ).start()
 
     scatter_in = (rsin1, rsin2)
 
-    def scatter_finish(stage, n):
-        drain(scatter_in[n].at[pl.ds(0, 15)], sem_rs.at[n])
-        total = stage[z, x]
+    def arrived(n, comp):
+        return scatter_in[n].at[comp, :, pl.ds(0, 40 if n and comp else 32)]
+
+    def scatter_finish(stage, n, comp):
+        drain(arrived(n, comp), sem_rs.at[n, comp])
+        height = 40 if n and comp else 32
+        total = stage[comp, z, x, 0:height]
         for j in range(15):
-            total = total + scatter_in[n][j]
+            total = total + scatter_in[n][comp, j, 0:height]
         return total
 
     rho = jnp.full((32, 128), pen_s[0], jnp.int32).astype(F32) / jnp.full((32, 128), pen_s[1], jnp.int32).astype(F32)
@@ -382,7 +389,7 @@
     compute(strip1)
     traded(2)
     traded(3)
-    scatter_start(acc1, sharein1, stage1, 0, rho, False)
+    scatter_start(acc1, sharein1, stage1, 0, rho)
 
     for d in range(1, 4):
         drain(posall.at[k, z], sem_ps.at[2 + d])
@@ -409,10 +416,9 @@
         wfull[b] = 1.0 / (dot(toeplitz, power[0]) + dot(toeplitz, power[1]) + rho[0:1])
     weight = own_weight()
 
-    total = scatter_finish(stage1, 0)
     for comp in range(2):
-        strip2[comp, pl.ds(own, TILE), :] = total[32 * comp : 32 * comp + 32] * weight
-    gather_start(strip2, 1)
+        strip2[comp, pl.ds(own, TILE), :] = scatter_finish(stage1, 0, comp) * weight
+        gather_start(strip2, 1, comp)
     for d in range(4):
         drain(nbuf.at[0], sem_ln.at[1, d])
     e = y * 2 + k
@@ -430,7 +436,7 @@
     gather_finish(strip2, 1)
 
     compute(strip2)
-    scatter_start(acc2, sharein2, stage2, 1, rho, True)
+    scatter_start(acc2, sharein2, stage2, 1, rho)
 
     for d in range(8):
         drain(nbuf.at[:, :, 0], sem_ln.at[2, d])
@@ -438,15 +444,14 @@
         qmat[h : h + 1, :] = qbuf[h // 32, h // 8 % 4, h // 4 % 2, h % 4]
     lines = qmat[...].T
 
-    total = scatter_finish(stage2, 1)
     for comp in range(2):
-        rows = slice(32 * comp, 32 * comp + 32)
-        qmsg[rows] = total[rows] * weight + mult_r[comp] / rho
-    qmsg[64:72] = total[64:72]
+        total = scatter_finish(stage2, 1, comp)
+        qmsg[32 * comp : 32 * comp + 32] = total[0:32] * weight + mult_r[comp] / rho
+    qmsg[64:72] = total[32:40]
     for comp in range(2):
         for i in range(32):
             qflip[32 * comp + 31 - i : 32 * comp + 32 - i] = qmsg[32 * comp + i : 32 * comp + i + 1]
-    qflip[64:72] = total[64:72]
+    qflip[64:72] = total[32:40]
     for u in fours:
         to = device(3 - z, u // 2 * 2 + 1 - k, 3 - x, u % 2)
         remote(qflip, qall.at[4 + y], sem_q_s.at[0], sem_q, to).start()
@@ -497,7 +502,8 @@
     for n, strip in ((0, strip1), (1, strip2)):
         drain(strip.at[0, pl.ds(0, 960)], sem_ag_s.at[n])
         drain(strip.at[0], sem_sh_s.at[n])
-        drain(scatter_in[n].at[pl.ds(0, 15)], sem_rs_s.at[n])
+        for comp in range(2):
+            drain(arrived(n, comp), sem_rs_s.at[n, comp])
         drain((sharein1, sharein2)[n], sem_acc_s.at[n])
     for d in range(3):
         drain(posr, sem_ps_s.at[d])
@@ -518,15 +524,15 @@
     scratch = [
         pltpu.VMEM((2, TOTAL, ROWS), F32),
         pltpu.VMEM((2, TOTAL, ROWS), F32),
-        pltpu.VMEM((2, 4, 2, 128, 128), F32),
-        pltpu.VMEM((2, 4, 2, 128, 128), F32),
+        pltpu.VMEM((2, 2, 4, 128, 128), F32),
+        pltpu.VMEM((2, 2, 4, 128, 128), F32),
         pltpu.VMEM((SCANS, 2, 384, 128), F32),
-        pltpu.VMEM((4, 2, 128, 128), F32),
-        pltpu.VMEM((4, 2, 128, 128), F32),
-        pltpu.VMEM((4, 4, 64, 128), F32),
-        pltpu.VMEM((4, 4, 72, 128), F32),
-        pltpu.VMEM((16, 64, 128), F32),
-        pltpu.VMEM((16, 72, 128), F32),
+        pltpu.VMEM((2, 4, 128, 128), F32),
+        pltpu.VMEM((2, 4, 128, 128), F32),
+        pltpu.VMEM((2, 4, 4, 32, 128), F32),
+        pltpu.VMEM((2, 4, 4, 40, 128), F32),
+        pltpu.VMEM((2, 15, 32, 128), F32),
+        pltpu.VMEM((2, 15, 40, 128), F32),
         pltpu.VMEM((SCANS, 128, 128), F32),
         pltpu.VMEM((SCANS // 2, 128, 256), F32),
         pltpu.VMEM((2, 128, 128), F32),
@@ -552,14 +558,14 @@
         pltpu.VMEM((72, 128), F32),
         pltpu.VMEM((8, 72, 128), F32),
         dma((5,)), dma((5,)), dma((2,)), dma((8,)),
-        dma((2,)), dma((2, 15)), dma((2,)), dma((2,)),
-        dma((2,)), dma((2, 4)), dma((2,)), dma((2,)),
+        dma((2,)), dma((2, 2, 15)), dma((2,)), dma((2,)),
+        dma((2,)), dma((2, 2)), dma((2, 2)), dma((2, 2)),
         dma((3, 8)), dma((3, 8)), dma((8,)), dma((8,)),
         dma((3,)), dma, dma,
     ]
     fresh, renewed = pl.pallas_call(
         kernel,
-        out_shape=(out, out),
+        out_shape=(pltpu.VMEM((2, TILE, ROWS), F32), pltpu.VMEM((2, TILE, ROWS), F32)),
         in_specs=[smem, smem, smem] + [any_] * 7,
         out_specs=(vmem, vmem),
         scratch_shapes=scratch,

time: 74.7 us -> 67.7 us (0.906); the launches traced: 73.3 us -> 67.2 us
  Pallas kernels: 69.9 us -> 65.3 us
  local copies, waits for them, and re-layouts: 2.75 us -> 1.23 us
    pallas_call x1, Pallas kernels: 69.9 us -> 65.3 us  [shards(): pl.pallas_call(kernel, out_shape=(pltpu.VMEM((2, TILE, ROWS), F32), pltpu...]
    unnamed x2, local copies, waits for them, and re-layouts: 2.75 us -> 1.23 us
where the time goes in v2:
time: 67.7 us; the launch traced here: 67.2 us
  Pallas kernels  65.3 us (96%)
  local copies, waits for them, and re-layouts  1.23 us (2%)
    pallas_call x1, Pallas kernels, shards(): pl.pallas_call(kernel, out_shape=(pltpu.VMEM((2, TILE, ROWS), F32), pltpu...  65.3 us

profile of v2, /device:TPU:9, one launch (start us, length us, event | category | flops | bytes accessed | tf_op | source)
XLA Modules:
  0.0 67.2 jit_solution(1862797224849217535)
XLA Ops:
  0.6 65.3 %shard_map.113 = (f32[2,32,128]{2,1,0:T(8,128)S(1)}, f32[2,32,128]{2,1,0:T(8,128)S(1)}) custom-call(s32[1,8]{1,0:T(1,128)} %pos_s.1, s32[4]{0:T(128)} %ang_s.1, s32[2]{0:T(128)} %pen_s.1, f32[2,32,128]{2,1,0:T(8,128)} %bitcast.21, f32[2,128,128]{2,1,0:T(8,128)} %probe_h.1, f32[8,128,128]{2,1,0:T(8,128)} %bitcast.20, f32[2,32,128]{2,1,0:T(8,128)} %bitcast.22, ...), custom_call_target="tpu_custom_call" | custom-call | tf_op jit(solution)/shard_map/pallas_call | solution.py:566
  65.9 0.6 copy.14
  66.6 0.6 copy.15

commit v3 on v2

--- a/solution.py
+++ b/solution.py
@@ -73,9 +73,9 @@
 
 
 def kernel(
-    pos_s, ang_s, pen_s, obj_h, probe_h, amp_h, prev_h, mult_h, vol_h, mat_h,
+    pos_h, ang_h, pen_h, obj_h, probe_h, amp_h, prev_h, mult_h, vol_h, mat_h,
     fresh_o, renew_o,
-    strip1, strip2, acc1, acc2, zbuf, sharein1, sharein2, stage1, stage2, rsin1, rsin2,
+    pos_s, ang_s, pen_s, strip1, strip2, acc1, acc2, zbuf, sharein1, sharein2, stage1, stage2, rsin1, rsin2,
     amp_r, amp_t, probe_v, probe_t, prev_r, mult_r, vol_v, mat_v,
     posb, posr, posall, posm, sums, flips, lbuf, mbuf, nbuf, qbuf, qmat, wfull, vec, qmsg, qflip, qall,
     sem_swap, sem_swap_send, sem_loc, sem_vol, sem_ag_s, sem_ag, sem_sh_s, sem_sh, sem_acc_s, sem_acc,
@@ -108,15 +108,6 @@
     def peer(dz, dx):
         return device((z + dz) % 4, y, (x + dx) % 4, k)
 
-    loc = [local(probe_h, probe_v, sem_loc.at[0]), local(mat_h, mat_v, sem_loc.at[1])]
-    vols = [
-        local(vol_h.at[comp, pl.ds(256 * q, 256)], vol_v.at[comp, pl.ds(256 * q, 256)], sem_vol.at[comp * 4 + q])
-        for comp in range(2)
-        for q in fours
-    ]
-    for copy in loc + vols:
-        copy.start()
-
     barrier = pltpu.get_barrier_semaphore()
     greeted = 0
     for dz, dx in PEERS:
@@ -132,6 +123,42 @@
                     barrier, inc=1, device_id=device(3 - z, (y + dy) % 4, 3 - x, (k + dk) % 2), device_id_type=MESH
                 )
                 greeted += 2
+    loc = [local(probe_h, probe_v, sem_loc.at[0]), local(mat_h, mat_v, sem_loc.at[1])]
+    scalars = [
+        local(src, dst, sem_loc.at[2 + i])
+        for i, (src, dst) in enumerate(((pos_h, pos_s), (ang_h, ang_s), (pen_h, pen_s)))
+    ]
+    vols = [
+        local(vol_h.at[comp], vol_v.at[comp], sem_vol.at[comp])
+        for comp in range(2)
+    ]
+    for copy in scalars + loc + vols:
+        copy.start()
+
+    pl.semaphore_wait(barrier, greeted)
+
+    trades = [
+        (obj_h, strip1.at[:, pl.ds(given, TILE)], strip1.at[:, pl.ds(own, TILE)]),
+        (posb, posr, posr),
+        (prev_h, prev_r, prev_r),
+        (mult_h, mult_r, mult_r),
+        (amp_h, amp_r, amp_r),
+    ]
+
+    def start_trade(i):
+        src, there, here = trades[i]
+
+        @pl.when(swapped)
+        def _():
+            remote(src, there, sem_swap_send.at[i], sem_swap.at[i], partner).start()
+
+        @pl.when(jnp.logical_not(swapped))
+        def _():
+            local(src, here, sem_swap.at[i]).start()
+
+    start_trade(0)
+    for copy in scalars:
+        copy.wait()
     for p in range(SCANS):
         posb[p : p + 1, :] = jnp.full((1, 128), pos_s[0, p], jnp.int32)
     zeros = jnp.zeros((128, 128), F32)
@@ -139,28 +166,7 @@
         for comp in range(2):
             zbuf[s, comp, 0:128] = zeros
             zbuf[s, comp, 256:384] = zeros
-    pl.semaphore_wait(barrier, greeted)
-
-    trades = [
-        (obj_h, strip1.at[:, pl.ds(given, TILE)], strip1.at[:, pl.ds(own, TILE)]),
-        (posb, posr, posr),
-        (prev_h, prev_r, prev_r),
-        (mult_h, mult_r, mult_r),
-        (amp_h, amp_r, amp_r),
-    ]
-
-    def start_trade(i):
-        src, there, here = trades[i]
-
-        @pl.when(swapped)
-        def _():
-            remote(src, there, sem_swap_send.at[i], sem_swap.at[i], partner).start()
-
-        @pl.when(jnp.logical_not(swapped))
-        def _():
-            local(src, here, sem_swap.at[i]).start()
-
-    for i in range(4):
+    for i in range(1, 4):
         start_trade(i)
 
     def traded(i):
@@ -170,8 +176,8 @@
 
     def volume_sums(comp):
         col = jnp.zeros((8, 1024), F32)
+        vols[comp].wait()
         for q in fours:
-            vols[comp * 4 + q].wait()
             for half in range(2):
                 def body(i, carry):
                     col, part = carry
@@ -196,17 +202,19 @@
     def gather_start(strip, n, comp):
         mine = strip.at[comp, pl.ds(own, TILE)]
         for j, (dz, dx) in enumerate(PEERS):
-            remote(mine, mine, sem_ag_s.at[n], sem_ag.at[n, comp, j], peer(dz, dx)).start()
+            remote(mine, mine, sem_ag_s.at[n], sem_ag.at[comp, (j + 1) // 2], peer(dz, dx)).start()
         remote(mine, mine, sem_sh_s.at[n], sem_sh.at[n], twin).start()
 
     def gather_finish(strip, n):
         for comp in range(2):
-            for j in reversed(range(15)):
-                dz, dx = PEERS[j]
-                src = (z - dz + 4) % 4 * 8 + k * 4 + (x - dx + 4) % 4
-                part = strip.at[comp, pl.ds(pl.multiple_of(src * TILE, TILE), TILE)]
-                drain(part, sem_ag.at[n, comp, j])
-                remote(part, part, sem_sh_s.at[n], sem_sh.at[n], twin).start()
+            for g in reversed(range(8)):
+                members = [0] if g == 0 else [2 * g - 1, 2 * g]
+                drain(strip.at[comp, pl.ds(0, TILE * len(members))], sem_ag.at[comp, g])
+                for j in members:
+                    dz, dx = PEERS[j]
+                    src = (z - dz + 4) % 4 * 8 + k * 4 + (x - dx + 4) % 4
+                    part = strip.at[comp, pl.ds(pl.multiple_of(src * TILE, TILE), TILE)]
+                    remote(part, part, sem_sh_s.at[n], sem_sh.at[n], twin).start()
         drain(strip.at[0], sem_sh.at[n])
 
     traded(0)
@@ -217,9 +225,9 @@
     traded(1)
     to_smem = local(posr, posm, sem_smem)
     to_smem.start()
-    local(posr, posall.at[k, z, x], sem_ps.at[6]).start()
+    local(posr, posall.at[k, z, x], sem_ps.at[0]).start()
     for d in range(1, 4):
-        remote(posr, posall.at[k, z, x], sem_ps_s.at[d - 1], sem_ps.at[d - 1], peer(0, d)).start()
+        remote(posr, posall.at[k, z, x], sem_ps_s.at[0], sem_ps.at[0], peer(0, d)).start()
 
     volume_sums(1)
 
@@ -258,10 +266,10 @@
             for b in range(8):
                 e = (u // 2 * 2 + b % 2) * 2 + u % 2
                 lbuf[j, b // 2, e] = rows[b : b + 1]
-    local(lbuf.at[x], mbuf.at[x], sem_ln.at[0, 3]).start()
+    local(lbuf.at[x], mbuf.at[x], sem_ln.at[0]).start()
     for d in range(1, 4):
         xd = (x + d) % 4
-        remote(lbuf.at[xd], mbuf.at[x], sem_ln_s.at[0, d - 1], sem_ln.at[0, d - 1], peer(0, d)).start()
+        remote(lbuf.at[xd], mbuf.at[x], sem_ln_s.at[0], sem_ln.at[0], peer(0, d)).start()
 
     for copy in loc:
         copy.wait()
@@ -271,11 +279,9 @@
 
     gather_finish(strip1, 0)
 
+    drain(posall.at[k, z], sem_ps.at[0])
     for d in range(1, 4):
-        drain(posr, sem_ps.at[d - 1])
-    drain(posr, sem_ps.at[6])
-    for d in range(1, 4):
-        remote(posall.at[k, z], posall.at[k, z], sem_ps_s.at[2 + d], sem_ps.at[2 + d], peer(d, 0)).start()
+        remote(posall.at[k, z], posall.at[k, z], sem_ps_s.at[1], sem_ps.at[1], peer(d, 0)).start()
 
     pr, pi = probe_t[0], probe_t[1]
 
@@ -284,44 +290,60 @@
         amp_t[s // 2, :, (s % 2) * 128 : (s % 2) * 128 + 128] = amp_r[s].T
 
     def compute(strip):
-        forward = (mat_v[0, 0], mat_v[0, 1])
-        inverse = (mat_v[1, 0], mat_v[1, 1])
         pr, pi = probe_t[0], probe_t[1]
 
-        def pair(p, carry):
-            exits = []
+        def right_apply(parts, m):
+            out = []
+            for u in parts:
+                hi, lo = split(u)
+                both = dot(jnp.concatenate([hi, lo], axis=0), mat_v[m, 0])
+                out.append(both[:256] + (both[256:] + dot(hi, mat_v[m, 1])))
+            return out
+
+        def left_apply(m, v):
+            hi, lo = split(v)
+            both = dot(jnp.concatenate([mat_v[m, 0], mat_v[m, 1]], axis=0), hi)
+            return both[:256] + (both[256:] + dot(mat_v[m, 0], lo))
+
+        def exits(p):
+            out = []
             for i in range(2):
                 start = posm[2 * p + i, 0]
                 wr = strip[0, pl.ds(start, 128), :]
                 wi = strip[1, pl.ds(start, 128), :]
-                exits.append(jnp.concatenate([pr * wr - pi * wi, pr * wi + pi * wr], axis=1))
-            a = dot3(split(jnp.concatenate(exits, axis=0)), forward)
-            a = jnp.concatenate(
+                out.append(jnp.concatenate([pr * wr - pi * wi, pr * wi + pi * wr], axis=1))
+            return jnp.concatenate(out, axis=0)
+
+        def turn(v):
+            return jnp.concatenate(
                 [
-                    jnp.concatenate([a[:128, :128], a[128:, :128]], axis=1),
-                    jnp.concatenate([a[:128, 128:], a[128:, 128:]], axis=1),
+                    jnp.concatenate([v[:128, :128], v[128:, :128]], axis=1),
+                    jnp.concatenate([v[:128, 128:], v[128:, 128:]], axis=1),
                 ],
                 axis=0,
             )
-            f = dot3(inverse, split(a))
+
+        def constrain(p, f):
             fr, fi = f[:128], f[128:]
             g = amp_t[p] * lax.rsqrt(jnp.maximum(fr * fr + fi * fi, FLOOR * FLOOR))
-            h = dot3(forward, split(jnp.concatenate([fr * g, fi * g], axis=0)))
-            h = jnp.concatenate(
-                [
-                    jnp.concatenate([h[:128, :128], h[128:, :128]], axis=1),
-                    jnp.concatenate([h[:128, 128:], h[128:, 128:]], axis=1),
-                ],
-                axis=0,
-            )
-            b = dot3(split(h), inverse)
+            return jnp.concatenate([fr * g, fi * g], axis=0)
+
+        def keep(p, v):
             for i in range(2):
-                br, bi = b[128 * i : 128 * i + 128, :128], b[128 * i : 128 * i + 128, 128:]
+                br, bi = v[128 * i : 128 * i + 128, :128], v[128 * i : 128 * i + 128, 128:]
                 zbuf[2 * p + i, 0, 128:256] = pr * br + pi * bi
                 zbuf[2 * p + i, 1, 128:256] = pr * bi - pi * br
-            return carry
-
-        lax.fori_loop(0, SCANS // 2, pair, 0, unroll=True)
+
+        for first in range(0, SCANS // 2, 4):
+            group = range(first, first + 4)
+            v = [exits(p) for p in group]
+            v = right_apply(v, 0)
+            v = [left_apply(1, turn(u)) for u in v]
+            v = [constrain(p, u) for p, u in zip(group, v)]
+            v = [left_apply(0, u) for u in v]
+            v = right_apply([turn(u) for u in v], 1)
+            for p, u in zip(group, v):
+                keep(p, u)
 
     def own_weight():
         return wfull[role // 4, pl.ds(pl.multiple_of(role % 4 * 32, 32), 32), :]
@@ -391,17 +413,15 @@
     traded(3)
     scatter_start(acc1, sharein1, stage1, 0, rho)
 
-    for d in range(1, 4):
-        drain(posall.at[k, z], sem_ps.at[2 + d])
-    remote(posall.at[k], posall.at[k], sem_ps_s.at[6], sem_ps.at[7], twin).start()
-    for d in range(4):
-        drain(mbuf.at[0], sem_ln.at[0, d])
-    local(mbuf.at[:, z], nbuf.at[z], sem_ln.at[1, 3]).start()
+    drain(posall.at[k, pl.ds(0, 3)], sem_ps.at[1])
+    remote(posall.at[k], posall.at[k], sem_ps_s.at[2], sem_ps.at[2], twin).start()
+    drain(mbuf, sem_ln.at[0])
+    local(mbuf.at[:, z], nbuf.at[z], sem_ln.at[1]).start()
     for d in range(1, 4):
         zd = (z + d) % 4
-        remote(mbuf.at[:, zd], nbuf.at[z], sem_ln_s.at[1, d - 1], sem_ln.at[1, d - 1], peer(d, 0)).start()
-
-    drain(posall.at[0], sem_ps.at[7])
+        remote(mbuf.at[:, zd], nbuf.at[z], sem_ln_s.at[1], sem_ln.at[1], peer(d, 0)).start()
+
+    drain(posall.at[0], sem_ps.at[2])
     where = posall[...].reshape(256, 128)
     lanes = lax.broadcasted_iota(jnp.int32, (256, 128), 1)
     high = jnp.where(lanes == (where >> 7), 1.0, 0.0)
@@ -419,57 +439,52 @@
     for comp in range(2):
         strip2[comp, pl.ds(own, TILE), :] = scatter_finish(stage1, 0, comp) * weight
         gather_start(strip2, 1, comp)
-    for d in range(4):
-        drain(nbuf.at[0], sem_ln.at[1, d])
+    drain(nbuf, sem_ln.at[1])
     e = y * 2 + k
-    local(nbuf.at[:, :, e], qbuf.at[yh * 2 + k, :, yl], sem_ln.at[2, 7]).start()
-    i = 0
+    local(nbuf.at[:, :, e], qbuf.at[yh * 2 + k, :, yl], sem_ln.at[2]).start()
     for dy in fours:
         for dk in range(2):
             if (dy, dk) != (0, 0):
                 yd, kd = (y + dy) % 4, (k + dk) % 2
                 remote(
                     nbuf.at[:, :, yd * 2 + kd], qbuf.at[yh * 2 + k, :, yl],
-                    sem_ln_s.at[2, i], sem_ln.at[2, i], device(z, yd, x, kd),
+                    sem_ln_s.at[2], sem_ln.at[2], device(z, yd, x, kd),
                 ).start()
-                i += 1
     gather_finish(strip2, 1)
 
     compute(strip2)
     scatter_start(acc2, sharein2, stage2, 1, rho)
 
-    for d in range(8):
-        drain(nbuf.at[:, :, 0], sem_ln.at[2, d])
+    drain(qbuf, sem_ln.at[2])
     for h in range(128):
         qmat[h : h + 1, :] = qbuf[h // 32, h // 8 % 4, h // 4 % 2, h % 4]
     lines = qmat[...].T
 
     for comp in range(2):
+        height = 40 if comp else 32
         total = scatter_finish(stage2, 1, comp)
-        qmsg[32 * comp : 32 * comp + 32] = total[0:32] * weight + mult_r[comp] / rho
-    qmsg[64:72] = total[32:40]
-    for comp in range(2):
+        qmsg[comp, 0:32] = total[0:32] * weight + mult_r[comp] / rho
         for i in range(32):
-            qflip[32 * comp + 31 - i : 32 * comp + 32 - i] = qmsg[32 * comp + i : 32 * comp + i + 1]
-    qflip[64:72] = total[32:40]
-    for u in fours:
-        to = device(3 - z, u // 2 * 2 + 1 - k, 3 - x, u % 2)
-        remote(qflip, qall.at[4 + y], sem_q_s.at[0], sem_q, to).start()
-    for i in range(3):
-        d = i + 1
-        yd, kd = ((yh + d // 2) % 2) * 2 + k, (k + d % 2) % 2
-        remote(qmsg, qall.at[y], sem_q_s.at[1], sem_q, device(z, yd, x, kd)).start()
-
-    @pl.when(swapped)
-    def _():
-        remote(qmsg, qall.at[y], sem_q_s.at[2], sem_q, device(z, yh * 2 + k, x, k)).start()
-
-    @pl.when(jnp.logical_not(swapped))
-    def _():
-        local(qmsg, qall.at[y], sem_q).start()
-
-    drain(qall, sem_q)
-    qs, qm = qall.at[pl.ds(0, 4)], qall.at[pl.ds(4, 4)]
+            qflip[comp, 31 - i : 32 - i] = qmsg[comp, i : i + 1]
+        if comp:
+            qmsg[comp, 32:40] = total[32:40]
+            qflip[comp, 32:40] = total[32:40]
+        part = pl.ds(0, height)
+        for u in fours:
+            to = device(3 - z, u // 2 * 2 + 1 - k, 3 - x, u % 2)
+            remote(qflip.at[comp, part], qall.at[comp, 4 + y, part], sem_q_s.at[comp], sem_q.at[comp], to).start()
+        mine = qmsg.at[comp, part], qall.at[comp, y, part]
+        for i in range(1, 4):
+            to = device(z, ((yh + i // 2) % 2) * 2 + k, x, (k + i % 2) % 2)
+            remote(*mine, sem_q_s.at[comp], sem_q.at[comp], to).start()
+
+        @pl.when(swapped)
+        def _():
+            remote(*mine, sem_q_s.at[comp], sem_q.at[comp], device(z, yh * 2 + k, x, k)).start()
+
+        @pl.when(jnp.logical_not(swapped))
+        def _():
+            local(*mine, sem_q.at[comp]).start()
 
     mine = ang_s[yh * 2 + k]
     same = [jnp.where(ang_s[u] == mine, 1.0, 0.0) for u in fours]
@@ -477,51 +492,58 @@
     other = [1.0 - same[u] - turned[u] for u in fours]
     members = same[0] + same[1] + same[2] + same[3] + turned[0] + turned[1] + turned[2] + turned[3]
     for comp in range(2):
-        rows = slice(32 * comp, 32 * comp + 32)
-        line = lines[rows]
+        drain(qall.at[comp, :, pl.ds(0, 40 if comp else 32)], sem_q.at[comp])
+    for comp in range(2):
+        line = lines[32 * comp : 32 * comp + 32]
         spread = (4.0 - members) * lines[64 + comp : 65 + comp]
         mix = members * line
+        keep = jnp.zeros((32, 128), F32)
         for u in fours:
-            mix = mix - same[u] * qs[u, rows] - turned[u] * qm[u, rows]
-            spread = spread - other[u] * (qs[u, 64 + comp : 65 + comp] + qm[u, 64 + comp : 65 + comp])
+            here, there = qall[comp, u, 0:32], qall[comp, 4 + u, 0:32]
+            mix = mix - same[u] * here - turned[u] * there
+            sums_u = qall[1, u, 32 + comp : 33 + comp] + qall[1, 4 + u, 32 + comp : 33 + comp]
+            spread = spread - other[u] * sums_u
+            keep = keep + jnp.where(yh * 2 + k == u, here, 0.0)
         fresh = line - 0.25 * (mix + spread * (1.0 / TOTAL))
         fresh_o[comp] = fresh
-        keep = jnp.zeros((32, 128), F32)
-        for u in fours:
-            keep = keep + jnp.where(yh * 2 + k == u, qs[u, rows], 0.0)
         renew_o[comp] = rho * (keep - fresh)
 
     @pl.when(swapped)
     def _():
         for i, (src, _, dst) in enumerate(trades):
             drain(dst, sem_swap_send.at[i])
-        drain(qmsg, sem_q_s.at[2])
-
-    drain(qs, sem_q_s.at[0])
-    drain(qs.at[pl.ds(0, 3)], sem_q_s.at[1])
+        for comp in range(2):
+            drain(qall.at[comp, :, pl.ds(0, 40 if comp else 32)], sem_q_s.at[comp])
+
+    @pl.when(jnp.logical_not(swapped))
+    def _():
+        for comp in range(2):
+            drain(qall.at[comp, pl.ds(0, 7), pl.ds(0, 40 if comp else 32)], sem_q_s.at[comp])
+
     for n, strip in ((0, strip1), (1, strip2)):
         drain(strip.at[0, pl.ds(0, 960)], sem_ag_s.at[n])
         drain(strip.at[0], sem_sh_s.at[n])
         for comp in range(2):
             drain(arrived(n, comp), sem_rs_s.at[n, comp])
         drain((sharein1, sharein2)[n], sem_acc_s.at[n])
-    for d in range(3):
-        drain(posr, sem_ps_s.at[d])
-        drain(posall.at[k, z], sem_ps_s.at[3 + d])
-        drain(lbuf.at[0], sem_ln_s.at[0, d])
-        drain(nbuf.at[0], sem_ln_s.at[1, d])
-    drain(posall.at[0], sem_ps_s.at[6])
-    for d in range(7):
-        drain(nbuf.at[:, :, 0], sem_ln_s.at[2, d])
+    drain(posall.at[0, 0, pl.ds(0, 3)], sem_ps_s.at[0])
+    drain(posall.at[0, pl.ds(0, 3)], sem_ps_s.at[1])
+    drain(posall.at[0], sem_ps_s.at[2])
+    drain(lbuf.at[pl.ds(0, 3)], sem_ln_s.at[0])
+    drain(nbuf.at[pl.ds(0, 3)], sem_ln_s.at[1])
+    drain(nbuf.at[:, :, pl.ds(0, 7)], sem_ln_s.at[2])
 
 
 def shards(objects, probe, positions, amplitudes, reproj_prev, multipliers, volume, angles, penalty):
     across = lambda a: jnp.transpose(a[0], (0, 2, 1))
-    any_, vmem, smem = (pl.BlockSpec(memory_space=m) for m in (pl.ANY, pltpu.VMEM, pltpu.SMEM))
+    any_, vmem = (pl.BlockSpec(memory_space=m) for m in (pl.ANY, pltpu.VMEM))
     mats = jnp.asarray(dft_matrices())
     dma = pltpu.SemaphoreType.DMA
     out = jax.ShapeDtypeStruct((2, TILE, ROWS), F32)
     scratch = [
+        pltpu.SMEM((1, SCANS), jnp.int32),
+        pltpu.SMEM((4,), jnp.int32),
+        pltpu.SMEM((2,), jnp.int32),
         pltpu.VMEM((2, TOTAL, ROWS), F32),
         pltpu.VMEM((2, TOTAL, ROWS), F32),
         pltpu.VMEM((2, 2, 4, 128, 128), F32),
@@ -554,19 +576,19 @@
         pltpu.VMEM((128, 128), F32),
         pltpu.VMEM((8, 128, 128), F32),
         pltpu.VMEM((8, 128), F32),
-        pltpu.VMEM((72, 128), F32),
-        pltpu.VMEM((72, 128), F32),
-        pltpu.VMEM((8, 72, 128), F32),
-        dma((5,)), dma((5,)), dma((2,)), dma((8,)),
-        dma((2,)), dma((2, 2, 15)), dma((2,)), dma((2,)),
+        pltpu.VMEM((2, 40, 128), F32),
+        pltpu.VMEM((2, 40, 128), F32),
+        pltpu.VMEM((2, 8, 40, 128), F32),
+        dma((5,)), dma((5,)), dma((5,)), dma((2,)),
+        dma((2,)), dma((2, 8)), dma((2,)), dma((2,)),
         dma((2,)), dma((2, 2)), dma((2, 2)), dma((2, 2)),
-        dma((3, 8)), dma((3, 8)), dma((8,)), dma((8,)),
-        dma((3,)), dma, dma,
+        dma((3,)), dma((3,)), dma((3,)), dma((3,)),
+        dma((2,)), dma((2,)), dma,
     ]
     fresh, renewed = pl.pallas_call(
         kernel,
         out_shape=(pltpu.VMEM((2, TILE, ROWS), F32), pltpu.VMEM((2, TILE, ROWS), F32)),
-        in_specs=[smem, smem, smem] + [any_] * 7,
+        in_specs=[any_] * 10,
         out_specs=(vmem, vmem),
         scratch_shapes=scratch,
         compiler_params=pltpu.CompilerParams(

time: 67.7 us -> 61.1 us (0.903)
  Pallas kernels: 65.3 us -> 59 us
    pallas_call x1, Pallas kernels: 65.3 us -> 59 us  [shards(): pl.pallas_call(kernel, out_shape=(pltpu.VMEM((2, TILE, ROWS), F32), pltpu...]
where the time goes in v3:
time: 61.1 us; the launch traced here: 60.8 us
  Pallas kernels  59 us (97%)
  local copies, waits for them, and re-layouts  1.23 us (2%)
  between operations  0.64 us (1%)
    pallas_call x1, Pallas kernels, shards(): pl.pallas_call(kernel, out_shape=(pltpu.VMEM((2, TILE, ROWS), F32), pltpu...  59 us
    unnamed x2, local copies, waits for them, and re-layouts  1.23 us

profile of v3, /device:TPU:9, one launch (start us, length us, event | category | flops | bytes accessed | tf_op | source)
XLA Modules:
  0.0 60.8 jit_solution(17492623100434072996)
XLA Ops:
  0.6 59.0 %shard_map.113 = (f32[2,32,128]{2,1,0:T(8,128)S(1)}, f32[2,32,128]{2,1,0:T(8,128)S(1)}) custom-call(s32[1,8]{1,0:T(1,128)} %pos_h.1, s32[4]{0:T(128)} %ang_h.1, s32[2]{0:T(128)} %pen_h.1, f32[2,32,128]{2,1,0:T(8,128)} %bitcast.21, f32[2,128,128]{2,1,0:T(8,128)} %probe_h.1, f32[8,128,128]{2,1,0:T(8,128)} %bitcast.20, f32[2,32,128]{2,1,0:T(8,128)} %bitcast.22, ...), custom_call_target="tpu_custom_call" | custom-call | tf_op jit(solution)/shard_map/pallas_call | solution.py:588
  59.6 0.6 %copy.14 = f32[1,2,128,32]{2,3,1,0:T(8,128)} copy(f32[1,2,128,32]{2,3,1,0:T(8,128)S(1)} %bitcast.18) | data formatting | bytes 65536
  60.2 0.6 %copy.15 = f32[1,2,128,32]{2,3,1,0:T(8,128)} copy(f32[1,2,128,32]{2,3,1,0:T(8,128)S(1)} %bitcast.17) | data formatting | bytes 65536

commit v4 on v3

--- a/solution.py
+++ b/solution.py
@@ -74,12 +74,12 @@
 
 def kernel(
     pos_h, ang_h, pen_h, obj_h, probe_h, amp_h, prev_h, mult_h, vol_h, mat_h,
-    fresh_o, renew_o,
+    line_o, change_o, renew_o,
     pos_s, ang_s, pen_s, strip1, strip2, acc1, acc2, zbuf, sharein1, sharein2, stage1, stage2, rsin1, rsin2,
     amp_r, amp_t, probe_v, probe_t, prev_r, mult_r, vol_v, mat_v,
     posb, posr, posall, posm, sums, flips, lbuf, mbuf, nbuf, qbuf, qmat, wfull, vec, qmsg, qflip, qall,
     sem_swap, sem_swap_send, sem_loc, sem_vol, sem_ag_s, sem_ag, sem_sh_s, sem_sh, sem_acc_s, sem_acc,
-    sem_rs_s, sem_rs, sem_ln_s, sem_ln, sem_ps_s, sem_ps, sem_q_s, sem_q, sem_smem,
+    sem_rs_s, sem_rs, sem_ln_s, sem_ln, sem_ps_s, sem_ps, sem_q_s, sem_q, sem_smem, sem_ring,
 ):
     view = lax.axis_index("view")
     tile = lax.axis_index("tile")
@@ -109,20 +109,13 @@
         return device((z + dz) % 4, y, (x + dx) % 4, k)
 
     barrier = pltpu.get_barrier_semaphore()
-    greeted = 0
-    for dz, dx in PEERS:
-        pl.semaphore_signal(barrier, inc=1, device_id=peer(dz, dx), device_id_type=MESH)
-        greeted += 1
-    for dy in fours:
+    near = [peer(0, d) for d in (2, 1, 3)] + [peer(d, 0) for d in (2, 1, 3)]
+    for dy in (2, 1, 3, 0):
         for dk in range(2):
             if (dy, dk) != (0, 0):
-                pl.semaphore_signal(
-                    barrier, inc=1, device_id=device(z, (y + dy) % 4, x, (k + dk) % 2), device_id_type=MESH
-                )
-                pl.semaphore_signal(
-                    barrier, inc=1, device_id=device(3 - z, (y + dy) % 4, 3 - x, (k + dk) % 2), device_id_type=MESH
-                )
-                greeted += 2
+                near.append(device(z, (y + dy) % 4, x, (k + dk) % 2))
+    for to in near:
+        pl.semaphore_signal(barrier, inc=1, device_id=to, device_id_type=MESH)
     loc = [local(probe_h, probe_v, sem_loc.at[0]), local(mat_h, mat_v, sem_loc.at[1])]
     scalars = [
         local(src, dst, sem_loc.at[2 + i])
@@ -135,7 +128,7 @@
     for copy in scalars + loc + vols:
         copy.start()
 
-    pl.semaphore_wait(barrier, greeted)
+    pl.semaphore_wait(barrier, len(near))
 
     trades = [
         (obj_h, strip1.at[:, pl.ds(given, TILE)], strip1.at[:, pl.ds(own, TILE)]),
@@ -157,6 +150,8 @@
             local(src, here, sem_swap.at[i]).start()
 
     start_trade(0)
+    for d in (2, 1, 3):
+        pl.semaphore_signal(sem_ring, inc=1, device_id=peer(0, d), device_id_type=MESH)
     for copy in scalars:
         copy.wait()
     for p in range(SCANS):
@@ -197,7 +192,6 @@
         for b in range(8):
             sums[2 * comp, b : b + 1, :] = jnp.sum(col[:, 128 * b : 128 * b + 128], axis=0, keepdims=True)
 
-    volume_sums(0)
 
     def gather_start(strip, n, comp):
         mine = strip.at[comp, pl.ds(own, TILE)]
@@ -217,6 +211,7 @@
                     remote(part, part, sem_sh_s.at[n], sem_sh.at[n], twin).start()
         drain(strip.at[0], sem_sh.at[n])
 
+    pl.semaphore_wait(sem_ring, 3)
     traded(0)
     for comp in range(2):
         gather_start(strip1, 0, comp)
@@ -229,11 +224,172 @@
     for d in range(1, 4):
         remote(posr, posall.at[k, z, x], sem_ps_s.at[0], sem_ps.at[0], peer(0, d)).start()
 
-    volume_sums(1)
-
-    flat = sums[...].reshape(32, 128)
     rr = lax.broadcasted_iota(jnp.int32, (128, 128), 0)
     cc = lax.broadcasted_iota(jnp.int32, (128, 128), 1)
+    scale = 1.0 / math.sqrt(TOTAL)
+    for copy in loc:
+        copy.wait()
+    for comp in range(2):
+        probe_t[comp] = probe_v[comp].T
+    to_smem.wait()
+
+    volume_sums(0)
+    gather_finish(strip1, 0)
+
+    drain(posall.at[k, z], sem_ps.at[0])
+    for d in range(1, 4):
+        remote(posall.at[k, z], posall.at[k, z], sem_ps_s.at[1], sem_ps.at[1], peer(d, 0)).start()
+
+    pr, pi = probe_t[0], probe_t[1]
+
+    traded(4)
+    for s in range(SCANS):
+        amp_t[s // 2, :, (s % 2) * 128 : (s % 2) * 128 + 128] = amp_r[s].T
+
+    def compute(strip):
+        pr, pi = probe_t[0], probe_t[1]
+
+        def right_apply(parts, m):
+            out = []
+            for u in parts:
+                hi, lo = split(u)
+                both = dot(jnp.concatenate([hi, lo], axis=0), mat_v[m, 0])
+                out.append(both[:256] + (both[256:] + dot(hi, mat_v[m, 1])))
+            return out
+
+        def left_apply(m, v):
+            hi, lo = split(v)
+            both = dot(jnp.concatenate([mat_v[m, 0], mat_v[m, 1]], axis=0), hi)
+            return both[:256] + (both[256:] + dot(mat_v[m, 0], lo))
+
+        def exits(p):
+            out = []
+            for i in range(2):
+                start = posm[2 * p + i, 0]
+                wr = strip[0, pl.ds(start, 128), :]
+                wi = strip[1, pl.ds(start, 128), :]
+                out.append(jnp.concatenate([pr * wr - pi * wi, pr * wi + pi * wr], axis=1))
+            return jnp.concatenate(out, axis=0)
+
+        def turn(v):
+            return jnp.concatenate(
+                [
+                    jnp.concatenate([v[:128, :128], v[128:, :128]], axis=1),
+                    jnp.concatenate([v[:128, 128:], v[128:, 128:]], axis=1),
+                ],
+                axis=0,
+            )
+
+        def constrain(p, f):
+            fr, fi = f[:128], f[128:]
+            g = amp_t[p] * lax.rsqrt(jnp.maximum(fr * fr + fi * fi, FLOOR * FLOOR))
+            return jnp.concatenate([fr * g, fi * g], axis=0)
+
+        def keep(p, v):
+            for i in range(2):
+                br, bi = v[128 * i : 128 * i + 128, :128], v[128 * i : 128 * i + 128, 128:]
+                zbuf[2 * p + i, 0, 128:256] = pr * br + pi * bi
+                zbuf[2 * p + i, 1, 128:256] = pr * bi - pi * br
+
+        for first in range(0, SCANS // 2, 4):
+            group = range(first, first + 4)
+            v = [exits(p) for p in group]
+            v = right_apply(v, 0)
+            v = [left_apply(1, turn(u)) for u in v]
+            v = [constrain(p, u) for p, u in zip(group, v)]
+            v = [left_apply(0, u) for u in v]
+            v = right_apply([turn(u) for u in v], 1)
+            for p, u in zip(group, v):
+                keep(p, u)
+
+    def own_weight():
+        return wfull[role // 4, pl.ds(pl.multiple_of(role % 4 * 32, 32), 32), :]
+
+    def block_sum(comp, b):
+        total = None
+        for s in range(SCANS):
+            off = jnp.clip(128 + 128 * b - posm[s, 0], 0, 256)
+            part = zbuf[s, comp, pl.ds(off, 128), :]
+            total = part if total is None else total + part
+        return total
+
+    def scatter_start(acc, sharein, stage, n, rho):
+        if n:
+            vec[...] = jnp.zeros((8, 128), F32)
+            for comp in range(2):
+                extra = mult_r[comp] / rho + (rho * prev_r[comp] - mult_r[comp]) * own_weight()
+                vec[comp : comp + 1, :] = jnp.sum(extra, axis=0, keepdims=True)
+
+        def blocks(comp, parity):
+            for j in fours:
+                i = 2 * j + parity
+                total = block_sum(comp, i)
+                acc[parity, comp, j] = total
+                if n:
+                    vec[comp : comp + 1, :] += jnp.sum(total * wfull[i], axis=0, keepdims=True)
+
+        for comp in range(2):
+            blocks(comp, 1 - k)
+            remote(acc.at[1 - k, comp], sharein.at[comp], sem_acc_s.at[n], sem_acc.at[n, comp], twin).start()
+        for comp in range(2):
+            blocks(comp, k)
+            drain(sharein.at[comp], sem_acc.at[n, comp])
+            for zd in fours:
+                for xd in fours:
+                    rows = slice(32 * xd, 32 * xd + 32)
+                    stage[comp, zd, xd, 0:32] = acc[k, comp, zd, rows] + sharein[comp, zd, rows]
+                    if n and comp:
+                        stage[comp, zd, xd, 32:40] = vec[...]
+            mine = pl.ds(0, 32)
+            stage[comp, z, x, mine] = stage[comp, z, x, mine] + (rho * prev_r[comp] - mult_r[comp])
+            height = 40 if n and comp else 32
+            for j, (dz, dx) in enumerate(PEERS):
+                remote(
+                    stage.at[comp, (z + dz) % 4, (x + dx) % 4, pl.ds(0, height)],
+                    scatter_in[n].at[comp, j, pl.ds(0, height)],
+                    sem_rs_s.at[n, comp], sem_rs.at[n, comp], peer(dz, dx),
+                ).start()
+
+    scatter_in = (rsin1, rsin2)
+
+    def arrived(n, comp):
+        return scatter_in[n].at[comp, :, pl.ds(0, 40 if n and comp else 32)]
+
+    def scatter_finish(stage, n, comp):
+        drain(arrived(n, comp), sem_rs.at[n, comp])
+        height = 40 if n and comp else 32
+        total = stage[comp, z, x, 0:height]
+        for j in range(15):
+            total = total + scatter_in[n][comp, j, 0:height]
+        return total
+
+    rho = jnp.full((32, 128), pen_s[0], jnp.int32).astype(F32) / jnp.full((32, 128), pen_s[1], jnp.int32).astype(F32)
+
+    compute(strip1)
+    traded(2)
+    traded(3)
+    scatter_start(acc1, sharein1, stage1, 0, rho)
+
+    drain(posall.at[k, pl.ds(0, 3)], sem_ps.at[1])
+    remote(posall.at[k], posall.at[k], sem_ps_s.at[2], sem_ps.at[2], twin).start()
+    drain(posall.at[0], sem_ps.at[2])
+    where = posall[...].reshape(256, 128)
+    lanes = lax.broadcasted_iota(jnp.int32, (256, 128), 1)
+    high = jnp.where(lanes == (where >> 7), 1.0, 0.0)
+    low = jnp.where(lanes == ((128 - (where & 127)) & 127), 1.0, 0.0)
+    counts = dot_tn(high.astype(BF16), low.astype(BF16))
+    power = split(pr * pr + pi * pi)
+    before = jnp.zeros((128, 128), F32)
+    for b in range(8):
+        here = pltpu.roll(jnp.broadcast_to(counts[b : b + 1], (128, 128)), 0, 1, stride=1, stride_axis=0)
+        toeplitz = jnp.where(rr >= cc, here, before).astype(BF16)
+        before = here
+        wfull[b] = 1.0 / (dot(toeplitz, power[0]) + dot(toeplitz, power[1]) + rho[0:1])
+    weight = own_weight()
+
+    volume_sums(1)
+
+    flat = sums[...].reshape(32, 128)
     anti = jnp.where(rr + cc == 127, 1.0, 0.0).astype(BF16)
     parts = split3(flat)
     turned = dot(parts[0], anti) + (dot(parts[1], anti) + dot(parts[2], anti))
@@ -271,174 +427,20 @@
         xd = (x + d) % 4
         remote(lbuf.at[xd], mbuf.at[x], sem_ln_s.at[0], sem_ln.at[0], peer(0, d)).start()
 
-    for copy in loc:
-        copy.wait()
     for comp in range(2):
-        probe_t[comp] = probe_v[comp].T
-    to_smem.wait()
-
-    gather_finish(strip1, 0)
-
-    drain(posall.at[k, z], sem_ps.at[0])
-    for d in range(1, 4):
-        remote(posall.at[k, z], posall.at[k, z], sem_ps_s.at[1], sem_ps.at[1], peer(d, 0)).start()
-
-    pr, pi = probe_t[0], probe_t[1]
-
-    traded(4)
-    for s in range(SCANS):
-        amp_t[s // 2, :, (s % 2) * 128 : (s % 2) * 128 + 128] = amp_r[s].T
-
-    def compute(strip):
-        pr, pi = probe_t[0], probe_t[1]
-
-        def right_apply(parts, m):
-            out = []
-            for u in parts:
-                hi, lo = split(u)
-                both = dot(jnp.concatenate([hi, lo], axis=0), mat_v[m, 0])
-                out.append(both[:256] + (both[256:] + dot(hi, mat_v[m, 1])))
-            return out
-
-        def left_apply(m, v):
-            hi, lo = split(v)
-            both = dot(jnp.concatenate([mat_v[m, 0], mat_v[m, 1]], axis=0), hi)
-            return both[:256] + (both[256:] + dot(mat_v[m, 0], lo))
-
-        def exits(p):
-            out = []
-            for i in range(2):
-                start = posm[2 * p + i, 0]
-                wr = strip[0, pl.ds(start, 128), :]
-                wi = strip[1, pl.ds(start, 128), :]
-                out.append(jnp.concatenate([pr * wr - pi * wi, pr * wi + pi * wr], axis=1))
-            return jnp.concatenate(out, axis=0)
-
-        def turn(v):
-            return jnp.concatenate(
-                [
-                    jnp.concatenate([v[:128, :128], v[128:, :128]], axis=1),
-                    jnp.concatenate([v[:128, 128:], v[128:, 128:]], axis=1),
-                ],
-                axis=0,
-            )
-
-        def constrain(p, f):
-            fr, fi = f[:128], f[128:]
-            g = amp_t[p] * lax.rsqrt(jnp.maximum(fr * fr + fi * fi, FLOOR * FLOOR))
-            return jnp.concatenate([fr * g, fi * g], axis=0)
-
-        def keep(p, v):
-            for i in range(2):
-                br, bi = v[128 * i : 128 * i + 128, :128], v[128 * i : 128 * i + 128, 128:]
-                zbuf[2 * p + i, 0, 128:256] = pr * br + pi * bi
-                zbuf[2 * p + i, 1, 128:256] = pr * bi - pi * br
-
-        for first in range(0, SCANS // 2, 4):
-            group = range(first, first + 4)
-            v = [exits(p) for p in group]
-            v = right_apply(v, 0)
-            v = [left_apply(1, turn(u)) for u in v]
-            v = [constrain(p, u) for p, u in zip(group, v)]
-            v = [left_apply(0, u) for u in v]
-            v = right_apply([turn(u) for u in v], 1)
-            for p, u in zip(group, v):
-                keep(p, u)
-
-    def own_weight():
-        return wfull[role // 4, pl.ds(pl.multiple_of(role % 4 * 32, 32), 32), :]
-
-    def block_sum(comp, b):
-        total = None
-        for s in range(SCANS):
-            off = jnp.clip(128 + 128 * b - posm[s, 0], 0, 256)
-            part = zbuf[s, comp, pl.ds(off, 128), :]
-            total = part if total is None else total + part
-        return total
-
-    def scatter_start(acc, sharein, stage, n, rho):
-        if n:
-            vec[...] = jnp.zeros((8, 128), F32)
-            for comp in range(2):
-                extra = mult_r[comp] / rho + (rho * prev_r[comp] - mult_r[comp]) * own_weight()
-                vec[comp : comp + 1, :] = jnp.sum(extra, axis=0, keepdims=True)
-
-        def blocks(comp, parity):
-            for j in fours:
-                i = 2 * j + parity
-                total = block_sum(comp, i)
-                acc[parity, comp, j] = total
-                if n:
-                    vec[comp : comp + 1, :] += jnp.sum(total * wfull[i], axis=0, keepdims=True)
-
-        for comp in range(2):
-            blocks(comp, 1 - k)
-            remote(acc.at[1 - k, comp], sharein.at[comp], sem_acc_s.at[n], sem_acc.at[n, comp], twin).start()
-        for comp in range(2):
-            blocks(comp, k)
-            drain(sharein.at[comp], sem_acc.at[n, comp])
-            for zd in fours:
-                for xd in fours:
-                    rows = slice(32 * xd, 32 * xd + 32)
-                    stage[comp, zd, xd, 0:32] = acc[k, comp, zd, rows] + sharein[comp, zd, rows]
-                    if n and comp:
-                        stage[comp, zd, xd, 32:40] = vec[...]
-            mine = pl.ds(0, 32)
-            stage[comp, z, x, mine] = stage[comp, z, x, mine] + (rho * prev_r[comp] - mult_r[comp])
-            height = 40 if n and comp else 32
-            for j, (dz, dx) in enumerate(PEERS):
-                remote(
-                    stage.at[comp, (z + dz) % 4, (x + dx) % 4, pl.ds(0, height)],
-                    scatter_in[n].at[comp, j, pl.ds(0, height)],
-                    sem_rs_s.at[n, comp], sem_rs.at[n, comp], peer(dz, dx),
-                ).start()
-
-    scatter_in = (rsin1, rsin2)
-
-    def arrived(n, comp):
-        return scatter_in[n].at[comp, :, pl.ds(0, 40 if n and comp else 32)]
-
-    def scatter_finish(stage, n, comp):
-        drain(arrived(n, comp), sem_rs.at[n, comp])
-        height = 40 if n and comp else 32
-        total = stage[comp, z, x, 0:height]
-        for j in range(15):
-            total = total + scatter_in[n][comp, j, 0:height]
-        return total
-
-    rho = jnp.full((32, 128), pen_s[0], jnp.int32).astype(F32) / jnp.full((32, 128), pen_s[1], jnp.int32).astype(F32)
-
-    compute(strip1)
-    traded(2)
-    traded(3)
-    scatter_start(acc1, sharein1, stage1, 0, rho)
-
-    drain(posall.at[k, pl.ds(0, 3)], sem_ps.at[1])
-    remote(posall.at[k], posall.at[k], sem_ps_s.at[2], sem_ps.at[2], twin).start()
+        strip2[comp, pl.ds(own, TILE), :] = scatter_finish(stage1, 0, comp) * weight
+        gather_start(strip2, 1, comp)
     drain(mbuf, sem_ln.at[0])
     local(mbuf.at[:, z], nbuf.at[z], sem_ln.at[1]).start()
     for d in range(1, 4):
         zd = (z + d) % 4
         remote(mbuf.at[:, zd], nbuf.at[z], sem_ln_s.at[1], sem_ln.at[1], peer(d, 0)).start()
 
-    drain(posall.at[0], sem_ps.at[2])
-    where = posall[...].reshape(256, 128)
-    lanes = lax.broadcasted_iota(jnp.int32, (256, 128), 1)
-    high = jnp.where(lanes == (where >> 7), 1.0, 0.0)
-    low = jnp.where(lanes == ((128 - (where & 127)) & 127), 1.0, 0.0)
-    counts = dot_tn(high.astype(BF16), low.astype(BF16))
-    power = split(pr * pr + pi * pi)
-    before = jnp.zeros((128, 128), F32)
-    for b in range(8):
-        here = pltpu.roll(jnp.broadcast_to(counts[b : b + 1], (128, 128)), 0, 1, stride=1, stride_axis=0)
-        toeplitz = jnp.where(rr >= cc, here, before).astype(BF16)
-        before = here
-        wfull[b] = 1.0 / (dot(toeplitz, power[0]) + dot(toeplitz, power[1]) + rho[0:1])
-    weight = own_weight()
-
-    for comp in range(2):
-        strip2[comp, pl.ds(own, TILE), :] = scatter_finish(stage1, 0, comp) * weight
-        gather_start(strip2, 1, comp)
+    gather_finish(strip2, 1)
+
+    compute(strip2)
+    scatter_start(acc2, sharein2, stage2, 1, rho)
+
     drain(nbuf, sem_ln.at[1])
     e = y * 2 + k
     local(nbuf.at[:, :, e], qbuf.at[yh * 2 + k, :, yl], sem_ln.at[2]).start()
@@ -450,16 +452,6 @@
                     nbuf.at[:, :, yd * 2 + kd], qbuf.at[yh * 2 + k, :, yl],
                     sem_ln_s.at[2], sem_ln.at[2], device(z, yd, x, kd),
                 ).start()
-    gather_finish(strip2, 1)
-
-    compute(strip2)
-    scatter_start(acc2, sharein2, stage2, 1, rho)
-
-    drain(qbuf, sem_ln.at[2])
-    for h in range(128):
-        qmat[h : h + 1, :] = qbuf[h // 32, h // 8 % 4, h // 4 % 2, h % 4]
-    lines = qmat[...].T
-
     for comp in range(2):
         height = 40 if comp else 32
         total = scatter_finish(stage2, 1, comp)
@@ -485,6 +477,11 @@
         @pl.when(jnp.logical_not(swapped))
         def _():
             local(*mine, sem_q.at[comp]).start()
+
+    drain(qbuf, sem_ln.at[2])
+    for h in range(128):
+        qmat[h : h + 1, :] = qbuf[h // 32, h // 8 % 4, h // 4 % 2, h % 4]
+    lines = qmat[...].T
 
     mine = ang_s[yh * 2 + k]
     same = [jnp.where(ang_s[u] == mine, 1.0, 0.0) for u in fours]
@@ -504,9 +501,10 @@
             sums_u = qall[1, u, 32 + comp : 33 + comp] + qall[1, 4 + u, 32 + comp : 33 + comp]
             spread = spread - other[u] * sums_u
             keep = keep + jnp.where(yh * 2 + k == u, here, 0.0)
-        fresh = line - 0.25 * (mix + spread * (1.0 / TOTAL))
-        fresh_o[comp] = fresh
-        renew_o[comp] = rho * (keep - fresh)
+        change = 0.25 * (mix + spread * (1.0 / TOTAL))
+        line_o[comp] = line
+        change_o[comp] = change
+        renew_o[comp] = rho * (keep - (line - change)) + change
 
     @pl.when(swapped)
     def _():
@@ -539,7 +537,6 @@
     any_, vmem = (pl.BlockSpec(memory_space=m) for m in (pl.ANY, pltpu.VMEM))
     mats = jnp.asarray(dft_matrices())
     dma = pltpu.SemaphoreType.DMA
-    out = jax.ShapeDtypeStruct((2, TILE, ROWS), F32)
     scratch = [
         pltpu.SMEM((1, SCANS), jnp.int32),
         pltpu.SMEM((4,), jnp.int32),
@@ -583,13 +580,13 @@
         dma((2,)), dma((2, 8)), dma((2,)), dma((2,)),
         dma((2,)), dma((2, 2)), dma((2, 2)), dma((2, 2)),
         dma((3,)), dma((3,)), dma((3,)), dma((3,)),
-        dma((2,)), dma((2,)), dma,
+        dma((2,)), dma((2,)), dma, pltpu.SemaphoreType.REGULAR,
     ]
-    fresh, renewed = pl.pallas_call(
+    line, change, renewed = pl.pallas_call(
         kernel,
-        out_shape=(pltpu.VMEM((2, TILE, ROWS), F32), pltpu.VMEM((2, TILE, ROWS), F32)),
+        out_shape=(pltpu.VMEM((2, TILE, ROWS), F32),) * 3,
         in_specs=[any_] * 10,
-        out_specs=(vmem, vmem),
+        out_specs=(vmem,) * 3,
         scratch_shapes=scratch,
         compiler_params=pltpu.CompilerParams(
             collective_id=0, has_side_effects=True, vmem_limit_bytes=60 * 1024 * 1024
@@ -607,7 +604,7 @@
         mats,
     )
     back = lambda a: jnp.transpose(a, (0, 2, 1))[None]
-    return back(fresh), back(renewed)
+    return back(line - change), back(renewed - change)
 
 
 def solution(mesh):

time: 61.1 us -> 58.1 us (0.951)
  Pallas kernels: 59 us -> 56.7 us
  local copies, waits for them, and re-layouts: 1.23 us -> 0 us
  other arithmetic: 0 us -> 0.64 us
    pallas_call x1, Pallas kernels: 59 us -> 56.7 us  [shards(): pl.pallas_call(kernel, out_shape=(pltpu.VMEM((2, TILE, ROWS), F32),) * 3,...]
    unnamed x2 -> x0, local copies, waits for them, and re-layouts: 1.23 us -> none
    broadcast_in_dim x0 -> x1, other arithmetic: none -> 0.64 us  [shards(): back = lambda a: jnp.transpose(a, (0, 2, 1))[None]]
where the time goes in v4:
time: 58.1 us; the launch traced here: 57.9 us
  Pallas kernels  56.7 us (98%)
  other arithmetic  0.64 us (1%)
  between operations  0.64 us (1%)
    pallas_call x1, Pallas kernels, shards(): pl.pallas_call(kernel, out_shape=(pltpu.VMEM((2, TILE, ROWS), F32),) * 3,...  56.7 us

profile of v4, /device:TPU:9, one launch (start us, length us, event | category | flops | bytes accessed | tf_op | source)
XLA Modules:
  0.0 57.9 jit_solution(15292171200641707405)
XLA Ops:
  0.6 56.7 %shard_map.113 = (f32[2,32,128]{2,1,0:T(8,128)S(1)}, f32[2,32,128]{2,1,0:T(8,128)S(1)}, f32[2,32,128]{2,1,0:T(8,128)S(1)}) custom-call(s32[1,8]{1,0:T(1,128)} %pos_h.1, s32[4]{0:T(128)} %ang_h.1, s32[2]{0:T(128)} %pen_h.1, f32[2,32,128]{2,1,0:T(8,128)} %bitcast.21, f32[2,128,128]{2,1,0:T(8,128)} %probe_h.1, f32[8,128,128]{2,1,0:T(8,128)} %bitcast.20, ...), custom_call_target="tpu_custom_call" | custom-call | tf_op jit(solution)/shard_map/pallas_call | solution.py:585
  57.3 0.6 %subtract_bitcast_fusion = (f32[1,2,128,32]{2,3,1,0:T(8,128)}, f32[1,2,128,32]{2,3,1,0:T(8,128)}) fusion(f32[2,32,128]{2,1,0:T(8,128)S(1)} %get-tuple-element.7, f32[2,32,128]{2,1,0:T(8,128)S(1)} %get-tuple-element.6, f32[2,32,128]{2,1,0:T(8,128)S(1)} %get-tuple-element.5), kind=kLoop, calls=%fused_computation | loop fusion | flops 16384 | bytes 163840 | tf_op jit(solution)/shard_map/broadcast_in_dim | solution.py:606

commit v5 on v4

--- a/solution.py
+++ b/solution.py
@@ -24,6 +24,8 @@
     [(dz, dx) for dz in range(4) for dx in range(4) if (dz, dx) != (0, 0)],
     key=lambda p: -(min(p[0], 4 - p[0]) + min(p[1], 4 - p[1])),
 )
+
+GROUP = (0, 0, 1, 1, 1, 2, 2, 2, 3, 3, 3, 4, 4, 4, 4)
 
 
 def dft_matrices():
@@ -78,8 +80,8 @@
     pos_s, ang_s, pen_s, strip1, strip2, acc1, acc2, zbuf, sharein1, sharein2, stage1, stage2, rsin1, rsin2,
     amp_r, amp_t, probe_v, probe_t, prev_r, mult_r, vol_v, mat_v,
     posb, posr, posall, posm, sums, flips, lbuf, mbuf, nbuf, qbuf, qmat, wfull, vec, qmsg, qflip, qall,
-    sem_swap, sem_swap_send, sem_loc, sem_vol, sem_ag_s, sem_ag, sem_sh_s, sem_sh, sem_acc_s, sem_acc,
-    sem_rs_s, sem_rs, sem_ln_s, sem_ln, sem_ps_s, sem_ps, sem_q_s, sem_q, sem_smem, sem_ring,
+    sem_swap, sem_swap_send, sem_loc, sem_vol, sem_out, sem_ag, sem_sh, sem_acc,
+    sem_rs_s, sem_rs, sem_small_s, sem_ln, sem_ps, sem_q_s, sem_q, sem_smem, sem_ring,
 ):
     view = lax.axis_index("view")
     tile = lax.axis_index("tile")
@@ -116,13 +118,13 @@
                 near.append(device(z, (y + dy) % 4, x, (k + dk) % 2))
     for to in near:
         pl.semaphore_signal(barrier, inc=1, device_id=to, device_id_type=MESH)
-    loc = [local(probe_h, probe_v, sem_loc.at[0]), local(mat_h, mat_v, sem_loc.at[1])]
+    loc = [local(probe_h, probe_v, sem_loc.at[3]), local(mat_h, mat_v, sem_loc.at[3])]
     scalars = [
-        local(src, dst, sem_loc.at[2 + i])
+        local(src, dst, sem_loc.at[i])
         for i, (src, dst) in enumerate(((pos_h, pos_s), (ang_h, ang_s), (pen_h, pen_s)))
     ]
     vols = [
-        local(vol_h.at[comp], vol_v.at[comp], sem_vol.at[comp])
+        local(vol_h.at[comp], vol_v.at[comp], sem_vol)
         for comp in range(2)
     ]
     for copy in scalars + loc + vols:
@@ -143,11 +145,11 @@
 
         @pl.when(swapped)
         def _():
-            remote(src, there, sem_swap_send.at[i], sem_swap.at[i], partner).start()
+            remote(src, there, sem_swap_send, sem_swap.at[i - i // 3], partner).start()
 
         @pl.when(jnp.logical_not(swapped))
         def _():
-            local(src, here, sem_swap.at[i]).start()
+            local(src, here, sem_swap.at[i - i // 3]).start()
 
     start_trade(0)
     for d in (2, 1, 3):
@@ -156,6 +158,7 @@
         copy.wait()
     for p in range(SCANS):
         posb[p : p + 1, :] = jnp.full((1, 128), pos_s[0, p], jnp.int32)
+    posb[SCANS:, :] = jnp.zeros((SCANS, 128), jnp.int32)
     zeros = jnp.zeros((128, 128), F32)
     for s in range(SCANS):
         for comp in range(2):
@@ -164,14 +167,18 @@
     for i in range(1, 4):
         start_trade(i)
 
-    def traded(i):
-        drain(trades[i][2], sem_swap.at[i])
+    def spare(rows):
+        return zbuf.at[0, 0, pl.ds(0, rows)] if rows < 384 else strip1.at[:, pl.ds(0, rows // 2)]
+
+    def traded(i, rows):
+        drain(spare(rows), sem_swap.at[i])
 
     ones8 = jnp.ones((8, 128), BF16)
 
     def volume_sums(comp):
         col = jnp.zeros((8, 1024), F32)
-        vols[comp].wait()
+        if comp == 0:
+            drain(vol_v, sem_vol)
         for q in fours:
             for half in range(2):
                 def body(i, carry):
@@ -196,39 +203,43 @@
     def gather_start(strip, n, comp):
         mine = strip.at[comp, pl.ds(own, TILE)]
         for j, (dz, dx) in enumerate(PEERS):
-            remote(mine, mine, sem_ag_s.at[n], sem_ag.at[comp, (j + 1) // 2], peer(dz, dx)).start()
-        remote(mine, mine, sem_sh_s.at[n], sem_sh.at[n], twin).start()
+            remote(mine, mine, sem_out, sem_ag.at[comp, GROUP[j]], peer(dz, dx)).start()
+        remote(mine, mine, sem_out, sem_sh, twin).start()
 
     def gather_finish(strip, n):
         for comp in range(2):
-            for g in reversed(range(8)):
-                members = [0] if g == 0 else [2 * g - 1, 2 * g]
+            for g in reversed(range(5)):
+                members = [j for j in range(15) if GROUP[j] == g]
                 drain(strip.at[comp, pl.ds(0, TILE * len(members))], sem_ag.at[comp, g])
                 for j in members:
                     dz, dx = PEERS[j]
                     src = (z - dz + 4) % 4 * 8 + k * 4 + (x - dx + 4) % 4
                     part = strip.at[comp, pl.ds(pl.multiple_of(src * TILE, TILE), TILE)]
-                    remote(part, part, sem_sh_s.at[n], sem_sh.at[n], twin).start()
-        drain(strip.at[0], sem_sh.at[n])
+                    remote(part, part, sem_out, sem_sh, twin).start()
+        if n == 0:
+            traded(3, 1024)
+            for s in range(SCANS):
+                amp_t[s // 2, :, (s % 2) * 128 : (s % 2) * 128 + 128] = amp_r[s].T
+        drain(strip.at[0], sem_sh)
 
     pl.semaphore_wait(sem_ring, 3)
-    traded(0)
+    traded(0, 64)
     for comp in range(2):
         gather_start(strip1, 0, comp)
     start_trade(4)
 
-    traded(1)
-    to_smem = local(posr, posm, sem_smem)
+    traded(1, 16)
+    mine = posr.at[pl.ds(0, SCANS)]
+    to_smem = local(mine, posm, sem_smem)
     to_smem.start()
-    local(posr, posall.at[k, z, x], sem_ps.at[0]).start()
+    local(mine, posall.at[k, z, x], sem_ps.at[0]).start()
     for d in range(1, 4):
-        remote(posr, posall.at[k, z, x], sem_ps_s.at[0], sem_ps.at[0], peer(0, d)).start()
+        remote(mine, posall.at[k, z, x], sem_small_s, sem_ps.at[0], peer(0, d)).start()
 
     rr = lax.broadcasted_iota(jnp.int32, (128, 128), 0)
     cc = lax.broadcasted_iota(jnp.int32, (128, 128), 1)
     scale = 1.0 / math.sqrt(TOTAL)
-    for copy in loc:
-        copy.wait()
+    drain(spare(1280), sem_loc.at[3])
     for comp in range(2):
         probe_t[comp] = probe_v[comp].T
     to_smem.wait()
@@ -238,13 +249,10 @@
 
     drain(posall.at[k, z], sem_ps.at[0])
     for d in range(1, 4):
-        remote(posall.at[k, z], posall.at[k, z], sem_ps_s.at[1], sem_ps.at[1], peer(d, 0)).start()
+        remote(posall.at[k, z], posall.at[k, z], sem_small_s, sem_ps.at[1], peer(d, 0)).start()
 
     pr, pi = probe_t[0], probe_t[1]
 
-    traded(4)
-    for s in range(SCANS):
-        amp_t[s // 2, :, (s % 2) * 128 : (s % 2) * 128 + 128] = amp_r[s].T
 
     def compute(strip):
         pr, pi = probe_t[0], probe_t[1]
@@ -320,8 +328,8 @@
                 extra = mult_r[comp] / rho + (rho * prev_r[comp] - mult_r[comp]) * own_weight()
                 vec[comp : comp + 1, :] = jnp.sum(extra, axis=0, keepdims=True)
 
-        def blocks(comp, parity):
-            for j in fours:
+        def blocks(comp, parity, part):
+            for j in part:
                 i = 2 * j + parity
                 total = block_sum(comp, i)
                 acc[parity, comp, j] = total
@@ -329,11 +337,16 @@
                     vec[comp : comp + 1, :] += jnp.sum(total * wfull[i], axis=0, keepdims=True)
 
         for comp in range(2):
-            blocks(comp, 1 - k)
-            remote(acc.at[1 - k, comp], sharein.at[comp], sem_acc_s.at[n], sem_acc.at[n, comp], twin).start()
+            for half in range(2):
+                part = pl.ds(2 * half, 2)
+                blocks(comp, 1 - k, (2 * half, 2 * half + 1))
+                remote(
+                    acc.at[1 - k, comp, part], sharein.at[comp, part], sem_out, sem_acc.at[comp], twin
+                ).start()
         for comp in range(2):
-            blocks(comp, k)
-            drain(sharein.at[comp], sem_acc.at[n, comp])
+            blocks(comp, k, fours)
+        for comp in range(2):
+            drain(sharein.at[comp], sem_acc.at[comp])
             for zd in fours:
                 for xd in fours:
                     rows = slice(32 * xd, 32 * xd + 32)
@@ -347,7 +360,7 @@
                 remote(
                     stage.at[comp, (z + dz) % 4, (x + dx) % 4, pl.ds(0, height)],
                     scatter_in[n].at[comp, j, pl.ds(0, height)],
-                    sem_rs_s.at[n, comp], sem_rs.at[n, comp], peer(dz, dx),
+                    sem_rs_s.at[n], sem_rs.at[comp], peer(dz, dx),
                 ).start()
 
     scatter_in = (rsin1, rsin2)
@@ -356,7 +369,7 @@
         return scatter_in[n].at[comp, :, pl.ds(0, 40 if n and comp else 32)]
 
     def scatter_finish(stage, n, comp):
-        drain(arrived(n, comp), sem_rs.at[n, comp])
+        drain(arrived(n, comp), sem_rs.at[comp])
         height = 40 if n and comp else 32
         total = stage[comp, z, x, 0:height]
         for j in range(15):
@@ -366,12 +379,11 @@
     rho = jnp.full((32, 128), pen_s[0], jnp.int32).astype(F32) / jnp.full((32, 128), pen_s[1], jnp.int32).astype(F32)
 
     compute(strip1)
-    traded(2)
-    traded(3)
+    traded(2, 128)
     scatter_start(acc1, sharein1, stage1, 0, rho)
 
     drain(posall.at[k, pl.ds(0, 3)], sem_ps.at[1])
-    remote(posall.at[k], posall.at[k], sem_ps_s.at[2], sem_ps.at[2], twin).start()
+    remote(posall.at[k], posall.at[k], sem_small_s, sem_ps.at[2], twin).start()
     drain(posall.at[0], sem_ps.at[2])
     where = posall[...].reshape(256, 128)
     lanes = lax.broadcasted_iota(jnp.int32, (256, 128), 1)
@@ -425,7 +437,7 @@
     local(lbuf.at[x], mbuf.at[x], sem_ln.at[0]).start()
     for d in range(1, 4):
         xd = (x + d) % 4
-        remote(lbuf.at[xd], mbuf.at[x], sem_ln_s.at[0], sem_ln.at[0], peer(0, d)).start()
+        remote(lbuf.at[xd], mbuf.at[x], sem_small_s, sem_ln.at[0], peer(0, d)).start()
 
     for comp in range(2):
         strip2[comp, pl.ds(own, TILE), :] = scatter_finish(stage1, 0, comp) * weight
@@ -434,7 +446,7 @@
     local(mbuf.at[:, z], nbuf.at[z], sem_ln.at[1]).start()
     for d in range(1, 4):
         zd = (z + d) % 4
-        remote(mbuf.at[:, zd], nbuf.at[z], sem_ln_s.at[1], sem_ln.at[1], peer(d, 0)).start()
+        remote(mbuf.at[:, zd], nbuf.at[z], sem_small_s, sem_ln.at[1], peer(d, 0)).start()
 
     gather_finish(strip2, 1)
 
@@ -450,7 +462,7 @@
                 yd, kd = (y + dy) % 4, (k + dk) % 2
                 remote(
                     nbuf.at[:, :, yd * 2 + kd], qbuf.at[yh * 2 + k, :, yl],
-                    sem_ln_s.at[2], sem_ln.at[2], device(z, yd, x, kd),
+                    sem_small_s, sem_ln.at[2], device(z, yd, x, kd),
                 ).start()
     for comp in range(2):
         height = 40 if comp else 32
@@ -464,15 +476,15 @@
         part = pl.ds(0, height)
         for u in fours:
             to = device(3 - z, u // 2 * 2 + 1 - k, 3 - x, u % 2)
-            remote(qflip.at[comp, part], qall.at[comp, 4 + y, part], sem_q_s.at[comp], sem_q.at[comp], to).start()
+            remote(qflip.at[comp, part], qall.at[comp, 4 + y, part], sem_q_s, sem_q.at[comp], to).start()
         mine = qmsg.at[comp, part], qall.at[comp, y, part]
         for i in range(1, 4):
             to = device(z, ((yh + i // 2) % 2) * 2 + k, x, (k + i % 2) % 2)
-            remote(*mine, sem_q_s.at[comp], sem_q.at[comp], to).start()
+            remote(*mine, sem_q_s, sem_q.at[comp], to).start()
 
         @pl.when(swapped)
         def _():
-            remote(*mine, sem_q_s.at[comp], sem_q.at[comp], device(z, yh * 2 + k, x, k)).start()
+            remote(*mine, sem_q_s, sem_q.at[comp], device(z, yh * 2 + k, x, k)).start()
 
         @pl.when(jnp.logical_not(swapped))
         def _():
@@ -508,28 +520,17 @@
 
     @pl.when(swapped)
     def _():
-        for i, (src, _, dst) in enumerate(trades):
-            drain(dst, sem_swap_send.at[i])
-        for comp in range(2):
-            drain(qall.at[comp, :, pl.ds(0, 40 if comp else 32)], sem_q_s.at[comp])
+        drain(spare(1232), sem_swap_send)
+        drain(spare(576), sem_q_s)
 
     @pl.when(jnp.logical_not(swapped))
     def _():
-        for comp in range(2):
-            drain(qall.at[comp, pl.ds(0, 7), pl.ds(0, 40 if comp else 32)], sem_q_s.at[comp])
-
-    for n, strip in ((0, strip1), (1, strip2)):
-        drain(strip.at[0, pl.ds(0, 960)], sem_ag_s.at[n])
-        drain(strip.at[0], sem_sh_s.at[n])
-        for comp in range(2):
-            drain(arrived(n, comp), sem_rs_s.at[n, comp])
-        drain((sharein1, sharein2)[n], sem_acc_s.at[n])
-    drain(posall.at[0, 0, pl.ds(0, 3)], sem_ps_s.at[0])
-    drain(posall.at[0, pl.ds(0, 3)], sem_ps_s.at[1])
-    drain(posall.at[0], sem_ps_s.at[2])
-    drain(lbuf.at[pl.ds(0, 3)], sem_ln_s.at[0])
-    drain(nbuf.at[pl.ds(0, 3)], sem_ln_s.at[1])
-    drain(nbuf.at[:, :, pl.ds(0, 7)], sem_ln_s.at[2])
+        drain(strip1.at[0, pl.ds(0, 504)], sem_q_s)
+
+    drain(zbuf.at[:, :, pl.ds(0, 376)], sem_out)
+    drain(spare(960), sem_rs_s.at[0])
+    drain(zbuf.at[pl.ds(0, 3), 0, pl.ds(0, 360)], sem_rs_s.at[1])
+    drain(strip1.at[0, pl.ds(0, 552)], sem_small_s)
 
 
 def shards(objects, probe, positions, amplitudes, reproj_prev, multipliers, volume, angles, penalty):
@@ -560,8 +561,8 @@
         pltpu.VMEM((2, TILE, ROWS), F32),
         pltpu.VMEM((2, TOTAL, TOTAL), F32),
         pltpu.VMEM((2, 2, 256, 256), BF16),
-        pltpu.VMEM((SCANS, 128), jnp.int32),
-        pltpu.VMEM((SCANS, 128), jnp.int32),
+        pltpu.VMEM((2 * SCANS, 128), jnp.int32),
+        pltpu.VMEM((2 * SCANS, 128), jnp.int32),
         pltpu.VMEM((2, 4, 4, SCANS, 128), jnp.int32),
         pltpu.SMEM((SCANS, 128), jnp.int32),
         pltpu.VMEM((4, 8, 128), F32),
@@ -576,11 +577,8 @@
         pltpu.VMEM((2, 40, 128), F32),
         pltpu.VMEM((2, 40, 128), F32),
         pltpu.VMEM((2, 8, 40, 128), F32),
-        dma((5,)), dma((5,)), dma((5,)), dma((2,)),
-        dma((2,)), dma((2, 8)), dma((2,)), dma((2,)),
-        dma((2,)), dma((2, 2)), dma((2, 2)), dma((2, 2)),
-        dma((3,)), dma((3,)), dma((3,)), dma((3,)),
-        dma((2,)), dma((2,)), dma, pltpu.SemaphoreType.REGULAR,
+        dma((4,)), dma, dma((4,)), dma, dma, dma((2, 5)), dma, dma((2,)),
+        dma((2,)), dma((2,)), dma, dma((3,)), dma((3,)), dma, dma((2,)), dma, pltpu.SemaphoreType.REGULAR,
     ]
     line, change, renewed = pl.pallas_call(
         kernel,

time: 58.1 us -> 57.9 us (level)
  no operation moved by 1% of the time
where the time goes in v5:
time: 57.9 us; the launch traced here: 57.6 us
  Pallas kernels  56.4 us (97%)
  other arithmetic  0.64 us (1%)
  between operations  0.64 us (1%)
    pallas_call x1, Pallas kernels, shards(): pl.pallas_call(kernel, out_shape=(pltpu.VMEM((2, TILE, ROWS), F32),) * 3,...  56.4 us

profile of v5, /device:TPU:9, one launch (start us, length us, event | category | flops | bytes accessed | tf_op | source)
XLA Modules:
  0.0 57.6 jit_solution(6923373418728781043)
XLA Ops:
  0.6 56.4 %shard_map.113 = (f32[2,32,128]{2,1,0:T(8,128)S(1)}, f32[2,32,128]{2,1,0:T(8,128)S(1)}, f32[2,32,128]{2,1,0:T(8,128)S(1)}) custom-call(s32[1,8]{1,0:T(1,128)} %pos_h.1, s32[4]{0:T(128)} %ang_h.1, s32[2]{0:T(128)} %pen_h.1, f32[2,32,128]{2,1,0:T(8,128)} %bitcast.21, f32[2,128,128]{2,1,0:T(8,128)} %probe_h.1, f32[8,128,128]{2,1,0:T(8,128)} %bitcast.20, ...), custom_call_target="tpu_custom_call" | custom-call | tf_op jit(solution)/shard_map/pallas_call | solution.py:583
  57.0 0.6 %subtract_bitcast_fusion = (f32[1,2,128,32]{2,3,1,0:T(8,128)}, f32[1,2,128,32]{2,3,1,0:T(8,128)}) fusion(f32[2,32,128]{2,1,0:T(8,128)S(1)} %get-tuple-element.7, f32[2,32,128]{2,1,0:T(8,128)S(1)} %get-tuple-element.6, f32[2,32,128]{2,1,0:T(8,128)S(1)} %get-tuple-element.5), kind=kLoop, calls=%fused_computation | loop fusion | flops 16384 | bytes 163840 | tf_op jit(solution)/shard_map/broadcast_in_dim | solution.py:604

commit v6 on v5

--- a/solution.py
+++ b/solution.py
@@ -333,8 +333,6 @@
                 i = 2 * j + parity
                 total = block_sum(comp, i)
                 acc[parity, comp, j] = total
-                if n:
-                    vec[comp : comp + 1, :] += jnp.sum(total * wfull[i], axis=0, keepdims=True)
 
         for comp in range(2):
             for half in range(2):
@@ -345,6 +343,12 @@
                 ).start()
         for comp in range(2):
             blocks(comp, k, fours)
+        if n:
+            for comp in range(2):
+                weighted = acc[k, comp, 0] * wfull[k] + acc[1 - k, comp, 0] * wfull[1 - k]
+                for j in range(1, 4):
+                    weighted += acc[k, comp, j] * wfull[2 * j + k] + acc[1 - k, comp, j] * wfull[2 * j + 1 - k]
+                vec[comp : comp + 1, :] += jnp.sum(weighted, axis=0, keepdims=True)
         for comp in range(2):
             drain(sharein.at[comp], sem_acc.at[comp])
             for zd in fours:
@@ -474,9 +478,6 @@
             qmsg[comp, 32:40] = total[32:40]
             qflip[comp, 32:40] = total[32:40]
         part = pl.ds(0, height)
-        for u in fours:
-            to = device(3 - z, u // 2 * 2 + 1 - k, 3 - x, u % 2)
-            remote(qflip.at[comp, part], qall.at[comp, 4 + y, part], sem_q_s, sem_q.at[comp], to).start()
         mine = qmsg.at[comp, part], qall.at[comp, y, part]
         for i in range(1, 4):
             to = device(z, ((yh + i // 2) % 2) * 2 + k, x, (k + i % 2) % 2)
@@ -489,6 +490,10 @@
         @pl.when(jnp.logical_not(swapped))
         def _():
             local(*mine, sem_q.at[comp]).start()
+
+        for u in fours:
+            to = device(3 - z, u // 2 * 2 + 1 - k, 3 - x, u % 2)
+            remote(qflip.at[comp, part], qall.at[comp, 4 + y, part], sem_q_s, sem_q.at[comp], to).start()
 
     drain(qbuf, sem_ln.at[2])
     for h in range(128):

time: 57.9 us -> 58.1 us (level)
  no operation moved by 1% of the time
where the time goes in v6:
time: 58.1 us; the launch traced here: 58 us
  Pallas kernels  56.7 us (98%)
  other arithmetic  0.64 us (1%)
  between operations  0.64 us (1%)
    pallas_call x1, Pallas kernels, shards(): pl.pallas_call(kernel, out_shape=(pltpu.VMEM((2, TILE, ROWS), F32),) * 3,...  56.7 us

profile of v6, /device:TPU:9, one launch (start us, length us, event | category | flops | bytes accessed | tf_op | source)
XLA Modules:
  0.0 58.0 jit_solution(16569611231162045274)
XLA Ops:
  0.6 56.7 %shard_map.113 = (f32[2,32,128]{2,1,0:T(8,128)S(1)}, f32[2,32,128]{2,1,0:T(8,128)S(1)}, f32[2,32,128]{2,1,0:T(8,128)S(1)}) custom-call(s32[1,8]{1,0:T(1,128)} %pos_h.1, s32[4]{0:T(128)} %ang_h.1, s32[2]{0:T(128)} %pen_h.1, f32[2,32,128]{2,1,0:T(8,128)} %bitcast.21, f32[2,128,128]{2,1,0:T(8,128)} %probe_h.1, f32[8,128,128]{2,1,0:T(8,128)} %bitcast.20, ...), custom_call_target="tpu_custom_call" | custom-call | tf_op jit(solution)/shard_map/pallas_call | solution.py:588
  57.4 0.6 %subtract_bitcast_fusion = (f32[1,2,128,32]{2,3,1,0:T(8,128)}, f32[1,2,128,32]{2,3,1,0:T(8,128)}) fusion(f32[2,32,128]{2,1,0:T(8,128)S(1)} %get-tuple-element.7, f32[2,32,128]{2,1,0:T(8,128)S(1)} %get-tuple-element.6, f32[2,32,128]{2,1,0:T(8,128)S(1)} %get-tuple-element.5), kind=kLoop, calls=%fused_computation | loop fusion | flops 16384 | bytes 163840 | tf_op jit(solution)/shard_map/broadcast_in_dim | solution.py:609
